TPU v7x, 32 devices: a whole 2x2x4 slice. The times are simulated.
32 devices in a mesh: view: 8 (over z, core), span: 4 (over y, x).
Axes of the slice: x: 2, y: 2, z: 4, core: 2. Of those that a mesh axis runs over, the one named last changes fastest.
Arguments:
- tokens: bfloat16 [8, 1024, 1024], P('view', 'span'), may hold values from -6 to 6
- scan_order: int32 [8, 1024], P('view'), may hold values from 0 to 1023, as said below
- w_merge: bfloat16 [4096, 1024], replicated, may hold values from -0.09375 to 0.09375
- bias: bfloat16 [1024], replicated, may hold values from -4 to 4
- cotangent: bfloat16 [8, 256, 1024], P('view', 'span'), may hold values from -6 to 6
Outputs:
- merged_out: bfloat16 [8, 256, 1024], P('view', 'span')
- token_grad: bfloat16 [8, 1024, 1024], P('view', 'span')
- weight_grad: float32 [4096, 1024], P(('view', 'span'))
- bias_grad: float32 [1024], replicated
Inputs may be any that keep to these rules, and one draw needn't show every extreme that they name: `scan_order`: each row is a permutation of the raster indices of one view. Call tokens 256 * b to 256 * (b + 1) - 1 band b, and scan positions 256 * c to 256 * (c + 1) - 1 block c: every block holds at most 96 tokens of any band, and in every row each block holds exactly 96 tokens of some band.
All inputs are finite; a program needn't handle non-finite values.
Results may differ from a plain program's by a relative error of at most 0.001.
Values may be sent and summed in bfloat16 or wider, within the bound.
No kernel may reach another device: no remote copies, remote signals or barrier semaphores. Data moves between devices by JAX's collectives and lax.ppermute only.
A program may use at most 128 MiB of HBM per device.

v0:
```python
import math

import jax
import jax.numpy as jnp
from jax import lax
from jax.sharding import PartitionSpec as P

COLS = 128


def body(tokens, scan_order, w_merge, bias, cotangent):
    spans = lax.axis_size("span")
    views = lax.axis_size("view")
    span_index = lax.axis_index("span")
    tok_dev = tokens.shape[1]
    width = tokens.shape[2]
    capacity = 3 * (tok_dev // spans) // 2
    rows_dev = tok_dev // COLS
    order_all = scan_order[0].reshape(spans, tok_dev)
    owners = order_all // tok_dev
    owner_hot = (owners[:, :, None] == jnp.arange(spans, dtype=jnp.int32)[None, None, :]).astype(
        jnp.int32
    )
    slot_rank = jnp.sum((jnp.cumsum(owner_hot, axis=1) - 1) * owner_hot, axis=2)
    dest_slots = owners * capacity + slot_rank
    my_slots = lax.dynamic_index_in_dim(dest_slots, span_index, 0, keepdims=False)
    outgoing = jnp.zeros((spans * capacity, width), jnp.bfloat16).at[my_slots].set(tokens[0])
    received = lax.all_to_all(
        outgoing.reshape(spans, capacity, width), "span", split_axis=0, concat_axis=0, tiled=True
    )
    arriving = owners == span_index
    source_slot = jnp.arange(spans, dtype=jnp.int32)[:, None] * capacity + slot_rank
    local_index = jnp.where(arriving, order_all - span_index * tok_dev, tok_dev)
    source_of = (
        jnp.zeros((tok_dev,), jnp.int32)
        .at[local_index.reshape(-1)]
        .set(source_slot.reshape(-1), mode="drop")
    )
    raster = received.reshape(spans * capacity, width)[source_of]
    merged = (
        raster.reshape(rows_dev // 2, 2, COLS // 2, 2, width)
        .transpose(0, 2, 1, 3, 4)
        .reshape(tok_dev // 4, 4 * width)
    )
    merged_out = (
        jnp.dot(merged, w_merge, preferred_element_type=jnp.float32) + bias.astype(jnp.float32)
    ).astype(jnp.bfloat16)
    grads = cotangent[0]
    grad_merged = lax.dot_general(
        grads, w_merge, (((1,), (1,)), ((), ())), preferred_element_type=jnp.float32
    ).astype(jnp.bfloat16)
    grad_raster = (
        grad_merged.reshape(rows_dev // 2, COLS // 2, 2, 2, width)
        .transpose(0, 2, 1, 3, 4)
        .reshape(tok_dev, width)
    )
    going_back = jnp.zeros((spans * capacity, width), jnp.bfloat16).at[source_of].set(grad_raster)
    returned = lax.all_to_all(
        going_back.reshape(spans, capacity, width), "span", split_axis=0, concat_axis=0, tiled=True
    )
    token_grad = returned.reshape(spans * capacity, width)[my_slots]
    kernel_rows = 4 * width
    merged_rows = merged.shape[0]
    group_rows = kernel_rows // (views * spans)
    regrouped = merged.reshape(merged_rows, views, spans, group_rows).transpose(0, 2, 1, 3)
    view_tokens = lax.all_to_all(regrouped, "span", split_axis=1, concat_axis=0, tiled=True)
    view_tokens = view_tokens.reshape(spans * merged_rows, views * group_rows)
    all_grads = lax.all_gather(grads, "span", axis=0, tiled=True)
    partial_sum = lax.dot_general(
        view_tokens, all_grads, (((0,), (0,)), ((), ())), preferred_element_type=jnp.float32
    )
    weight_sum = lax.psum_scatter(partial_sum, "view", scatter_dimension=0, tiled=True)
    bias_total = lax.psum(jnp.sum(grads.astype(jnp.float32), axis=0), ("view", "span"))
    grad_scale = 1.0 / math.sqrt(views * spans * (tok_dev // 4))
    return (merged_out[None], token_grad[None], weight_sum * grad_scale, bias_total * grad_scale)


def solution(mesh):
    in_specs = (P("view", "span", None), P("view", None), P(), P(), P("view", "span", None))
    out_specs = (P("view", "span", None), P("view", "span", None), P(("view", "span"), None), P())
    return jax.shard_map(body, mesh=mesh, in_specs=in_specs, out_specs=out_specs, check_vma=False)
```

profile of v0, /device:TPU:0, one launch (start us, length us, event | category | flops | bytes accessed | tf_op | source)
XLA Modules:
  0.0 131.2 jit_solution(6496516762859729099)
XLA Ops:
  7.2 0.0 copy-start
  7.2 0.0 copy-start.1
  7.2 0.8 and_select_fusion.1
  8.0 4.8 %reduce-window.6 = s32[4,4,2,128]{3,2,1,0:T(2,128)S(1)} reduce-window(s32[4,4,2,128]{3,2,1,0:T(2,128)S(1)} %compare_convert_fusion, s32[]{:T(128)} %constant.19.clone.1), window={size=1x1x1x128 pad=0_0x0_0x0_0x127_0}, to_apply=%region_0.1 | reduce-window | flops 520192 | bytes 32772 | tf_op jit(solution)/shard_map/reduce-window
  12.8 0.1 slice.12
  12.9 0.1 copy.16
  13.0 0.1 copy.17
  13.2 0.1 add_add_fusion
  13.3 0.5 broadcast.237
  13.8 1.3 %reduce.3 = s32[1024]{0:T(1024)S(1)} reduce(s32[1,1024]{1,0:T(1,128)} %param.6, s32[]{:T(128)} %broadcast.237), dimensions={0}, to_apply=%param.6.reduce_sub_computation.3 | reduce | bytes 8196 | tf_op args[1]
  15.2 0.0 copy-done
  15.2 2.6 %scatter_custom_fusion = bf16[384,1024]{1,0:T(8,128)(2,1)} fusion(s32[256]{0:T(256)S(1)} %bitcast.75, bf16[1,256,1024]{2,1,0:T(8,128)(2,1)S(1)} %copy-done, bf16[]{:T(256)} %constant.15.clone.1), kind=kCustom, calls=%fused_computation.13 | custom fusion | bytes 1310722 | tf_op jit(solution)/shard_map/scatter | solution.py:27
  17.8 5.2 %all-to-all-start = ((bf16[4,96,1024]{2,1,0:T(8,128)(2,1)}), bf16[4,96,1024]{2,1,0:T(8,128)(2,1)S(1)}, u32[]{:S(2)}, u32[]{:S(2)}) async-start(bf16[4,96,1024]{2,1,0:T(8,128)(2,1)} %bitcast.6), calls=%async_computation | async-start | bytes 1572864 | tf_op jit(solution)/shard_map/all_to_all | solution.py:28
  23.0 0.1 add_bitcast_fusion
  23.1 0.7 compare_select_fusion
  23.8 4.3 %scatter_custom_fusion.1 = s32[256]{0:T(256)S(1)} fusion(s32[1024]{0:T(1024)S(1)} %bitcast.78, s32[1024]{0:T(1024)S(1)} %bitcast.77, s32[]{:T(128)} %constant.19.clone.1), kind=kCustom, calls=%fused_computation.59 | custom fusion | bytes 1028 | tf_op jit(solution)/shard_map/scatter | solution.py:37
  28.2 5.7 %all-to-all-done = bf16[4,96,1024]{2,1,0:T(8,128)(2,1)S(1)} async-done(((bf16[4,96,1024]{2,1,0:T(8,128)(2,1)}), bf16[4,96,1024]{2,1,0:T(8,128)(2,1)S(1)}, u32[]{:S(2)}, u32[]{:S(2)}) %all-to-all-start) | async-done | bytes 786464 | tf_op jit(solution)/shard_map/all_to_all | solution.py:28
  33.8 1.2 gather_fusion
  35.0 0.2 reshape.224
  35.2 0.4 copy.30
  35.6 0.3 reshape_reshape.3
  35.9 0.9 copy.20
  36.8 3.5 %all-to-all-start.2 = ((bf16[64,4,8,128]{3,2,0,1:T(8,128)(2,1)}), bf16[64,4,8,128]{3,2,0,1:T(8,128)(2,1)S(1)}, u32[]{:S(2)}, u32[]{:S(2)}) async-start(bf16[64,4,8,128]{3,2,0,1:T(8,128)(2,1)} %copy.20), calls=%async_computation.2 | async-start | bytes 1048576 | tf_op jit(solution)/shard_map/all_to_all | solution.py:66
  40.3 0.0 reduce-scatter.2.cloned.1.call-start
  40.3 0.0 copy-done.1
  40.3 13.7 %all-gather = bf16[1,256,1024]{2,1,0:T(8,128)(2,1)S(1)} all-gather(bf16[1,64,1024]{2,1,0:T(8,128)(2,1)S(1)} %copy-done.1), channel_id=2, replica_groups=mesh['view'=8,'span'=4] {'span'}, dimensions={1}, use_global_device_ids=true | all-gather | bytes 655360 | tf_op jit(solution)/shard_map/all_gather | solution.py:68
  54.0 0.0 all-to-all-done.2
  54.0 2.7 %fusion.2 = f32[1024,1024]{1,0:T(8,128)} fusion(bf16[32,8,8,128]{3,2,1,0:T(8,128)(2,1)S(1)} %bitcast.70, bf16[1,256,1024]{2,1,0:T(8,128)(2,1)S(1)} %all-gather), kind=kOutput, calls=%fused_computation.9 | convolution fusion | flops 536870912 | bytes 5242880 | tf_op jit(solution)/shard_map/dot_general | solution.py:69
  56.7 0.0 copy-start.2
  56.7 0.0 reduce-scatter.2.cloned.1.call-update
  56.7 6.0 %convolution_convert_fusion = bf16[64,4096]{1,0:T(8,128)(2,1)S(1)} fusion(bf16[4096,1024]{1,0:T(8,128)(2,1)} %param.7, bf16[1,64,1024]{2,1,0:T(8,128)(2,1)S(1)} %copy-done.1), kind=kOutput, calls=%fused_computation.5 | convolution fusion | flops 537133056 | bytes 9043968 | tf_op jit(solution)/shard_map/dot_general | solution.py:49
  62.8 0.4 reshape.226
  63.1 0.4 copy.29
  63.5 0.2 reshape.267
  63.7 2.6 %scatter_custom_fusion.2 = bf16[384,1024]{1,0:T(8,128)(2,1)} fusion(s32[256]{0:T(256)S(1)} %compare_select_fusion.6, bf16[256,1024]{1,0:T(8,128)(2,1)S(1)} %reshape.267, bf16[]{:T(256)} %constant.15.clone.1), kind=kCustom, calls=%fused_computation.17 | custom fusion | bytes 786434 | tf_op jit(solution)/shard_map/scatter | solution.py:57
  66.3 3.5 %all-to-all-start.1 = ((bf16[4,96,1024]{2,1,0:T(8,128)(2,1)}), bf16[4,96,1024]{2,1,0:T(8,128)(2,1)S(1)}, u32[]{:S(2)}, u32[]{:S(2)}) async-start(bf16[4,96,1024]{2,1,0:T(8,128)(2,1)} %bitcast.14), calls=%async_computation.1 | async-start | bytes 1572864 | tf_op jit(solution)/shard_map/all_to_all | solution.py:58
  69.8 0.0 copy-done.2
  69.9 44.0 %psum.7 = f32[1024]{0:T(1024)S(1)} all-reduce(f32[1024]{0:T(1024)S(1)} %convert_reduce_fusion), channel_id=1, replica_groups=mesh['view'=8,'span'=4] {'view','span'}, use_global_device_ids=true, to_apply=%region_8.9 | all-reduce | flops 1024 | bytes 8192 | tf_op jit(solution)/shard_map/psum | solution.py:73
  113.8 0.6 broadcast_multiply_fusion.1
  114.4 0.4 reshape.225
  114.8 0.0 all-to-all-done.1
  114.8 2.0 %gather_fusion.1 = bf16[256,1024]{1,0:T(8,128)(2,1)} fusion(bf16[384,1024]{1,0:T(8,128)(2,1)S(1)} %bitcast.67, s32[1024]{0:T(1024)S(1)} %pad_clamp_fusion), kind=kCustom, calls=%fused_computation.1 | custom fusion | bytes 1049600 | tf_op jit(solution)/shard_map/gather | solution.py:61
  116.8 5.6 %fusion.1 = bf16[1,64,1024]{2,1,0:T(8,128)(2,1)} fusion(bf16[64,4096]{1,0:T(8,128)(2,1)S(1)} %reshape.225, bf16[4096,1024]{1,0:T(8,128)(2,1)} %param.7, f32[1024]{0:T(1024)S(1)} %convert_element_type.18), kind=kOutput, calls=%fused_computation.8 | convolution fusion | flops 537001984 | bytes 9048064 | tf_op jit(solution)/shard_map/dot_general | solution.py:46
  122.4 0.0 reduce-scatter.2.cloned.1.call-done
  122.4 1.9 %broadcast_multiply_fusion = f32[128,1024]{1,0:T(8,128)} fusion(f32[128,1024]{1,0:T(8,128)} %reduce-scatter.2.cloned.1.call-done), kind=kLoop, calls=%fused_computation.21 | loop fusion | flops 131072 | bytes 1048576 | tf_op jit(solution)/shard_map/mul | solution.py:75
  (15 shorter events, 0.2 us)
Async XLA Ops:
  7.2 8.1 %copy-start = (bf16[1,256,1024]{2,1,0:T(8,128)(2,1)S(1)}, bf16[1,256,1024]{2,1,0:T(8,128)(2,1)}, u32[]{:S(2)}) copy-start(bf16[1,256,1024]{2,1,0:T(8,128)(2,1)} %param.5) | copy-start | bytes 1572868
  7.2 33.1 %copy-start.1 = (bf16[1,64,1024]{2,1,0:T(8,128)(2,1)S(1)}, bf16[1,64,1024]{2,1,0:T(8,128)(2,1)}, u32[]{:S(2)}) copy-start(bf16[1,64,1024]{2,1,0:T(8,128)(2,1)} %param.9) | copy-start | bytes 393220
  17.8 16.0 %all-to-all-start = ((bf16[4,96,1024]{2,1,0:T(8,128)(2,1)}), bf16[4,96,1024]{2,1,0:T(8,128)(2,1)S(1)}, u32[]{:S(2)}, u32[]{:S(2)}) async-start(bf16[4,96,1024]{2,1,0:T(8,128)(2,1)} %bitcast.6), calls=%async_computation | async-start | bytes 1572864 | tf_op jit(solution)/shard_map/all_to_all | solution.py:28
  36.8 17.2 %all-to-all-start.2 = ((bf16[64,4,8,128]{3,2,0,1:T(8,128)(2,1)}), bf16[64,4,8,128]{3,2,0,1:T(8,128)(2,1)S(1)}, u32[]{:S(2)}, u32[]{:S(2)}) async-start(bf16[64,4,8,128]{3,2,0,1:T(8,128)(2,1)} %copy.20), calls=%async_computation.2 | async-start | bytes 1048576 | tf_op jit(solution)/shard_map/all_to_all | solution.py:66
  40.3 82.2 %reduce-scatter.2.cloned.1.call-start = ((), (), s32[]{:S(2)}) async-start(), calls=%async_computation.4 | async-start | bytes 4718592 | tf_op jit(solution)/shard_map/reduce_scatter | solution.py:72
  56.7 13.1 %copy-start.2 = (bf16[1024]{0:T(1024)(128)(2,1)S(1)}, bf16[1024]{0:T(1024)(128)(2,1)}, u32[]{:S(2)}) copy-start(bf16[1024]{0:T(1024)(128)(2,1)} %param.8) | copy-start | bytes 6148
  66.3 48.5 %all-to-all-start.1 = ((bf16[4,96,1024]{2,1,0:T(8,128)(2,1)}), bf16[4,96,1024]{2,1,0:T(8,128)(2,1)S(1)}, u32[]{:S(2)}, u32[]{:S(2)}) async-start(bf16[4,96,1024]{2,1,0:T(8,128)(2,1)} %bitcast.14), calls=%async_computation.1 | async-start | bytes 1572864 | tf_op jit(solution)/shard_map/all_to_all | solution.py:58
Sparse Core Ops, SparseCore 0:
  56.8 51.2 reduce-scatter.1
where the time goes:
time: 132 us; the launch traced here: 131 us
  blocking collectives  57.6 us (44%)
  local copies, waits for them, and re-layouts  16.6 us (13%)
  matrix products  14.3 us (11%)
  between operations  14.2 us (11%)
  starting transfers between devices  12.2 us (9%)
  other arithmetic  10.4 us (8%)
  waiting for transfers between devices  5.71 us (4%)
    psum x1, blocking collectives, body(): lax.psum(jnp.sum(grads.astype(jnp.float32), axis=0), ('view', 'span'))  44 us
    all_gather x1, blocking collectives, body(): all_grads = lax.all_gather(grads, 'span', axis=0, tiled=True)  13.7 us
    dot_general x1, matrix products, body(): lax.dot_general(grads, w_merge, (((1,), (1,)), ((), ())), preferred_eleme...  6.04 us
    all_to_all x1, waiting for transfers between devices, body(): lax.all_to_all(outgoing.reshape(spans, capacity, width), 'span', split_ax...  5.69 us
    dot_general x1, matrix products, body(): jnp.dot(merged, w_merge, preferred_element_type=jnp.float32)  5.61 us
    all_to_all x1, starting transfers between devices, body(): lax.all_to_all(outgoing.reshape(spans, capacity, width), 'span', split_ax...  5.19 us
    another operation x2, other arithmetic  4.84 us
    scatter x1, local copies, waits for them, and re-layouts, body(): source_of = jnp.zeros((tok_dev,), jnp.int32).at[local_index.reshape(-1)]....  4.3 us
  transfers between devices with their start and end apart: 4, of which 1 were waited for; matrix products, arithmetic and copies ran while one was open for 18% of the time, Pallas kernels for 0%

commit v1 on v0

--- a/solution.py
+++ b/solution.py
@@ -1,14 +1,23 @@
+import functools
 import math
 
 import jax
 import jax.numpy as jnp
 from jax import lax
+from jax.experimental import pallas as pl
+from jax.experimental.pallas import tpu as pltpu
 from jax.sharding import PartitionSpec as P
 
+
 COLS = 128
-
-
-def body(tokens, scan_order, w_merge, bias, cotangent):
+MERGE = 4
+SPANS = 4
+LANES = 128
+PACK_LIMIT = 32
+MAIN_LIMIT = 52
+
+
+def general_body(tokens, scan_order, w_merge, bias, cotangent):
     spans = lax.axis_size("span")
     views = lax.axis_size("view")
     span_index = lax.axis_index("span")
@@ -75,6 +84,316 @@
     return (merged_out[None], token_grad[None], weight_sum * grad_scale, bias_total * grad_scale)
 
 
+def xor_permute(x, axis, offset):
+    n = lax.axis_size(axis)
+    return lax.ppermute(x, axis, [(i, i ^ offset) for i in range(n)])
+
+
+def raster_of(k, band, local, tok_dev):
+    half = COLS // 2
+    row = local // half
+    col = local % half
+    return band * tok_dev + (2 * row + k // 2) * COLS + 2 * col + k % 2
+
+
+def order_row(order_ref, block, tok_dev):
+    return order_ref[:, pl.ds(pl.multiple_of(block * tok_dev, LANES), tok_dev)]
+
+
+def bf16_hot(mask):
+    return jnp.where(mask, 1.0, 0.0).astype(jnp.bfloat16)
+
+
+def rank_of(member):
+    n = member.shape[1]
+    upper = lax.broadcasted_iota(jnp.int32, (n, n), 0) <= lax.broadcasted_iota(jnp.int32, (n, n), 1)
+    rows = jnp.broadcast_to(bf16_hot(member), (16, n))
+    count = jnp.dot(rows, bf16_hot(upper), preferred_element_type=jnp.float32)
+    return count[:1].astype(jnp.int32) - 1
+
+
+def slot_hot(order, band, tok_dev, slots):
+    member = (order // tok_dev) == band
+    slot = lax.broadcasted_iota(jnp.int32, (slots, order.shape[1]), 0)
+    return jnp.where(member & (rank_of(member) == slot), 1.0, 0.0).astype(jnp.bfloat16)
+
+
+def pack_kernel(order_hbm, t_hbm, c_hbm, b_hbm, order_ref, t_ref, c_ref, b_ref, x1, x2, x3, p1, p2, p3,
+                sems):
+    tok_dev = t_ref.shape[0]
+    mrows = c_ref.shape[0]
+    group = LANES
+    s = lax.axis_index("span")
+    stride = group * SPANS
+    pairs = ((order_hbm, order_ref), (t_hbm, t_ref), (c_hbm, c_ref), (b_hbm, b_ref))
+    copies = [pltpu.make_async_copy(a, b, sems.at[i]) for i, (a, b) in enumerate(pairs)]
+    for copy in copies:
+        copy.start()
+    for copy in copies:
+        copy.wait()
+    x1[:mrows, :] = c_ref[...]
+    x2[:mrows, :] = c_ref[...]
+    for o, x, first in ((1, x1, mrows), (2, x2, mrows), (3, x3, 0)):
+        for c in range(2):
+            start = pl.multiple_of((s ^ o) * group + c * stride, LANES)
+            for j in range(MERGE):
+                column = (2 * j + c) * group
+                x[first:first + mrows, column:column + group] = t_ref[
+                    j * mrows:(j + 1) * mrows, pl.ds(start, group)
+                ]
+    order = order_row(order_ref, s, tok_dev)
+    for o, p in ((1, p1), (2, p2), (3, p3)):
+        hot = slot_hot(order, s ^ o, tok_dev, p.shape[0])
+        p[...] = jnp.dot(hot, t_ref[...], preferred_element_type=jnp.float32).astype(p.dtype)
+
+
+def select_kernel(order_ref, t_ref, x1, x2, x3, m0, m1, m2, m3):
+    tok_dev = t_ref.shape[0]
+    mrows = tok_dev // MERGE
+    group = LANES
+    stride = group * SPANS
+    s = lax.axis_index("span")
+    z = lax.axis_index("view") // 2
+    order = jnp.concatenate([order_row(order_ref, s ^ o, tok_dev) for o in range(SPANS)], axis=1)
+    starts = [pl.multiple_of(s * group + c * stride, LANES) for c in range(2)]
+    parts = [jnp.concatenate([t_ref[:, pl.ds(start, group)] for start in starts], axis=1)]
+    for x, first in ((x1, mrows), (x2, mrows), (x3, 0)):
+        parts += [
+            x[first:first + mrows, 2 * j * group:2 * (j + 1) * group] for j in range(MERGE)
+        ]
+    slab = jnp.concatenate(parts, axis=0)
+    target = lax.broadcasted_iota(jnp.int32, (tok_dev, 1), 0)
+    band = s ^ (target // mrows)
+    local = target % mrows
+    for dz, out in enumerate((m0, m1, m2, m3)):
+        raster = raster_of(z ^ dz, band, local, tok_dev)
+        hot = bf16_hot(raster == order)
+        out[...] = jnp.dot(hot, slab, preferred_element_type=jnp.float32).astype(out.dtype)
+
+
+def fetch(w_hbm, w_ref, sems, k):
+    width = w_ref.shape[1]
+    rows = pl.ds(pl.multiple_of(k * width, width), width)
+    return pltpu.make_async_copy(w_hbm.at[rows, :], w_ref.at[k], sems.at[k])
+
+
+def forward_kernel(order_ref, bias_ref, t_ref, p1, p2, p3, w_hbm, out, mine_ref, acc_ref, w_ref, sems):
+    tok_dev = t_ref.shape[0]
+    mrows = tok_dev // MERGE
+    s = lax.axis_index("span")
+    f32 = jnp.float32
+    for k in range(MERGE):
+        fetch(w_hbm, w_ref, sems, k).start()
+    local = lax.broadcasted_iota(jnp.int32, (tok_dev, 1), 0)
+    raster = raster_of(local // mrows, s, local % mrows, tok_dev)
+    mine_order = order_row(order_ref, s, tok_dev)
+    mine = jnp.dot(bf16_hot(raster == mine_order), t_ref[...], preferred_element_type=f32)
+    key = raster - s * tok_dev + 1
+    for o, p in ((1, p1), (2, p2), (3, p3)):
+        order = order_row(order_ref, s ^ o, tok_dev)
+        slots = slot_hot(order, s, tok_dev, p.shape[0])
+        place = jnp.where(order // tok_dev == s, order - s * tok_dev + 1, 0)
+        place = jnp.broadcast_to(place, (16, tok_dev)).astype(f32).astype(jnp.bfloat16)
+        held = lax.dot_general(place, slots, (((1,), (1,)), ((), ())), preferred_element_type=f32)
+        hot = bf16_hot(key == held[:1].astype(jnp.int32))
+        mine += jnp.dot(hot, p[...], preferred_element_type=f32)
+    mine_ref[...] = mine.astype(mine_ref.dtype)
+    acc_ref[...] = jnp.broadcast_to(bias_ref[...].astype(f32).reshape(1, -1), acc_ref.shape)
+
+    @pl.loop(0, MERGE)
+    def _(k):
+        fetch(w_hbm, w_ref, sems, k).wait()
+        rows = mine_ref[pl.ds(pl.multiple_of(k * mrows, mrows), mrows), :]
+        acc_ref[...] += jnp.dot(rows, w_ref[k], preferred_element_type=f32)
+
+    out[...] = acc_ref[...].astype(out.dtype)
+
+
+def backward_kernel(order_ref, c0, x1, x2, cda, cdb, w_hbm, tgrad, grads_ref, tacc_ref, w_ref, sems):
+    mrows = c0.shape[0]
+    tok_dev = MERGE * mrows
+    s = lax.axis_index("span")
+    f32 = jnp.float32
+    for k in range(MERGE):
+        fetch(w_hbm, w_ref, sems, k).start()
+    grads_ref[...] = jnp.concatenate(
+        [c0[...], x1[:mrows, :], x2[:mrows, :], cda[...], cdb[...]], axis=0
+    )
+    tacc_ref[...] = jnp.zeros_like(tacc_ref)
+    local = lax.broadcasted_iota(jnp.int32, (tok_dev, 1), 0)
+    band = s ^ (local // mrows)
+    order = order_row(order_ref, s, tok_dev)
+
+    @pl.loop(0, MERGE)
+    def _(k):
+        hot = bf16_hot(raster_of(k, band, local % mrows, tok_dev) == order)
+        picked = lax.dot_general(
+            hot, grads_ref[...], (((0,), (0,)), ((), ())), preferred_element_type=f32
+        ).astype(jnp.bfloat16)
+        fetch(w_hbm, w_ref, sems, k).wait()
+        tacc_ref[...] += lax.dot_general(
+            picked, w_ref[k], (((1,), (1,)), ((), ())), preferred_element_type=f32
+        )
+
+    tgrad[...] = tacc_ref[...].astype(tgrad.dtype)
+
+
+def weight_kernel(m0, m1, m2, m3, c0, e0, x1, ex, x2, ey, cda, cdb, eda, edb, keep, keep_bias, give):
+    mrows = c0.shape[0]
+    core = lax.axis_index("view") % 2
+    f32 = jnp.float32
+
+    def stacked(o):
+        return jnp.concatenate(
+            [m[o * mrows:(o + 1) * mrows, :] for m in (m0, m2, m1, m3)], axis=0
+        )
+
+    cx, cy = x1.at[:mrows], x2.at[:mrows]
+    blocks = [(c0, e0), (cx, ex), (cy, ey), (cda, cdb, eda, edb)]
+    lhs = jnp.concatenate([stacked(o) for o in range(len(blocks))], axis=0)
+    rhs = jnp.concatenate([r[...] for b in blocks for r in b], axis=0)
+    group = lhs.shape[1] // 2
+    total = lax.dot_general(lhs, rhs, (((0,), (0,)), ((), ())), preferred_element_type=f32)
+    low, high = total[:group], total[group:]
+    mine = core == 0
+    keep[...] = jnp.where(mine, low, high)
+    give[:group, :] = jnp.where(mine, high, low)
+    pieces = rhs.astype(f32).reshape(len(blocks), MERGE, mrows, rhs.shape[1])
+
+    def block_sum(b):
+        return (b[0] + b[2]) + (b[1] + b[3])
+
+    sums = [block_sum(pieces[o]) for o in range(len(blocks))]
+    tree = (sums[0] + sums[1]) + (sums[2] + sums[3])
+    bias = jnp.broadcast_to(jnp.sum(tree, axis=0, keepdims=True), keep_bias.shape)
+    keep_bias[...] = bias
+    give[group:, :] = bias
+
+
+def finish_kernel(scale, keep, keep_bias, taken, weight_grad, bias_grad):
+    group = keep.shape[0]
+    weight_grad[...] = (keep[...] + taken[:group, :]) * scale
+    bias_grad[...] = (keep_bias[:1, :] + taken[group:group + 1, :]) * scale
+
+
+def shape(rows, cols, dtype=jnp.bfloat16):
+    return jax.ShapeDtypeStruct((rows, cols), dtype)
+
+
+def call(kernel, args, outs, cost, hbm=(), scratch=(), limit=32):
+    vmem = pl.BlockSpec(memory_space=pltpu.VMEM)
+    far = pl.BlockSpec(memory_space=pltpu.HBM)
+    return pl.pallas_call(
+        kernel,
+        out_shape=outs,
+        in_specs=[far if i in hbm else vmem for i in range(len(args))],
+        out_specs=[vmem] * len(outs),
+        scratch_shapes=scratch,
+        cost_estimate=cost,
+        compiler_params=pltpu.CompilerParams(vmem_limit_bytes=int(limit * 1024 * 1024)),
+    )(*args)
+
+
+def cost_of(flops, moved):
+    return pl.CostEstimate(flops=flops, bytes_accessed=moved, transcendentals=0)
+
+
+def quad_steps(tokens, scan_order, w_merge, bias, cotangent):
+    spans = lax.axis_size("span")
+    views = lax.axis_size("view")
+    tok_dev = tokens.shape[1]
+    width = tokens.shape[2]
+    mrows = tok_dev // MERGE
+    group = MERGE * width // (views * spans)
+    capacity = 3 * (tok_dev // spans) // 2
+    f32 = jnp.float32
+    t0 = tokens[0]
+    c0 = cotangent[0]
+
+    half = mrows // 2
+    bf16 = jnp.bfloat16
+    order, tv, cv, bv, *sent = call(
+        pack_kernel,
+        (scan_order, t0, c0, bias),
+        [
+            shape(*scan_order.shape, jnp.int32),
+            shape(tok_dev, width),
+            shape(mrows, width),
+            jax.ShapeDtypeStruct(bias.shape, bias.dtype),
+        ]
+        + [shape(2 * mrows, width)] * 2
+        + [shape(mrows, width)]
+        + [shape(capacity, width)] * 3,
+        cost_of(2 * 3 * capacity * tok_dev * width, 4 * tok_dev * width),
+        hbm=(0, 1, 2, 3),
+        scratch=[pltpu.SemaphoreType.DMA((4,))],
+        limit=PACK_LIMIT,
+    )
+    x1, x2, x3 = [xor_permute(sent[o - 1], "span", o) for o in range(1, 4)]
+    c2 = xor_permute(c0, "view", 4)
+    ps = [xor_permute(sent[o + 2], "span", o) for o in range(1, 4)]
+    c13 = xor_permute(jnp.concatenate([cv, c2], axis=0), "view", 2)
+    extra = jnp.concatenate([c2, c13], axis=0)
+    cda = xor_permute(x1[:half], "span", 2)
+    cdb = xor_permute(x2[half:mrows], "span", 1)
+    ex = xor_permute(extra, "span", 1)
+    ey = xor_permute(extra, "span", 2)
+    ehalf = extra.shape[0] // 2
+    eda = xor_permute(ex[:ehalf], "span", 2)
+    edb = xor_permute(ey[ehalf:], "span", 1)
+    picks = call(
+        select_kernel,
+        (order, tv, x1, x2, x3),
+        [shape(tok_dev, 2 * group)] * MERGE,
+        cost_of(2 * spans * spans * tok_dev * tok_dev * 2 * group, 4 * tok_dev * width),
+    )
+    ms = [picks[0]] + [xor_permute(picks[dz], "view", 2 * dz) for dz in range(1, MERGE)]
+    weights = [pltpu.VMEM((MERGE, width, width), bf16), pltpu.SemaphoreType.DMA((MERGE,))]
+    (merged_out,) = call(
+        forward_kernel,
+        (order, bv, tv, *ps, w_merge),
+        [shape(mrows, width)],
+        cost_of(4 * tok_dev * width * width, 8 * width * width),
+        hbm=(6,),
+        scratch=[pltpu.VMEM((tok_dev, width), bf16), pltpu.VMEM((mrows, width), f32)] + weights,
+        limit=MAIN_LIMIT,
+    )
+    (token_grad,) = call(
+        backward_kernel,
+        (order, cv, x1, x2, cda, cdb, w_merge),
+        [shape(tok_dev, width)],
+        cost_of(10 * tok_dev * width * width, 8 * width * width),
+        hbm=(6,),
+        scratch=[pltpu.VMEM((tok_dev, width), bf16), pltpu.VMEM((tok_dev, width), f32)] + weights,
+        limit=MAIN_LIMIT,
+    )
+    keep, keep_bias, give = call(
+        weight_kernel,
+        (*ms, cv, extra, x1, ex, x2, ey, cda, cdb, eda, edb),
+        [shape(group, width, f32), shape(8, width, f32), shape(group + 8, width, f32)],
+        cost_of(4 * spans * tok_dev * group * width, 8 * tok_dev * width),
+    )
+    taken = xor_permute(give, "view", 1)
+    scale = 1.0 / math.sqrt(views * spans * mrows)
+    weight_grad, bias_grad = call(
+        functools.partial(finish_kernel, scale),
+        (keep, keep_bias, taken),
+        [shape(group, width, f32), shape(1, width, f32)],
+        cost_of(group * width, 12 * group * width),
+    )
+    return merged_out[None], token_grad[None], weight_grad, bias_grad[0]
+
+
+def body(tokens, scan_order, w_merge, bias, cotangent):
+    spans = lax.axis_size("span")
+    views = lax.axis_size("view")
+    width = tokens.shape[2]
+    group = MERGE * width // (views * spans)
+    if spans == SPANS and views == 2 * MERGE and group == LANES:
+        return quad_steps(tokens, scan_order, w_merge, bias, cotangent)
+    return general_body(tokens, scan_order, w_merge, bias, cotangent)
+
+
 def solution(mesh):
     in_specs = (P("view", "span", None), P("view", None), P(), P(), P("view", "span", None))
     out_specs = (P("view", "span", None), P("view", "span", None), P(("view", "span"), None), P())

time: 132 us -> 81.1 us (0.61)
  blocking collectives: 57.6 us -> 0 us
  waiting for transfers between devices: 5.71 us -> 37.1 us
  Pallas kernels: 0 us -> 15.1 us
  matrix products: 14.3 us -> 0 us
  between operations: 14.2 us -> 0.75 us
  local copies, waits for them, and re-layouts: 16.6 us -> 3.38 us
  starting transfers between devices: 12.2 us -> 24.5 us
  other arithmetic: 10.4 us -> 0.02 us
    psum x1 -> x0, blocking collectives: 44 us -> none  [body(): lax.psum(jnp.sum(grads.astype(jnp.float32), axis=0), ('view', 'span'))]
    ppermute x0 -> x18, waiting for transfers between devices: none -> 37.1 us  [xor_permute(): return lax.ppermute(x, axis, [(i, i ^ offset) for i in range(n)])]
    ppermute x0 -> x18, starting transfers between devices: none -> 24.5 us  [xor_permute(): return lax.ppermute(x, axis, [(i, i ^ offset) for i in range(n)])]
    pallas_call x0 -> x6, Pallas kernels: none -> 15.1 us  [call(): pl.pallas_call(kernel, out_shape=outs, in_specs=[far if i in hbm else vme...]
    dot_general x3 -> x0, matrix products: 14.3 us -> none  [the longest x1 6.04 us: body(): lax.dot_general(grads, w_merge, (((1,), (1,)), ((), ())), preferred_eleme...]
    all_gather x1 -> x0, blocking collectives: 13.7 us -> none  [body(): all_grads = lax.all_gather(grads, 'span', axis=0, tiled=True)]
    all_to_all x3 -> x0, starting transfers between devices: 12.2 us -> none  [the longest x1 5.19 us: body(): lax.all_to_all(outgoing.reshape(spans, capacity, width), 'span', split_ax...]
    scatter x3 -> x0, local copies, waits for them, and re-layouts: 9.49 us -> none  [the longest x1 4.3 us: body(): source_of = jnp.zeros((tok_dev,), jnp.int32).at[local_index.reshape(-1)]....]
  transfers between devices with their start and end apart: 4 -> 18, of which waited for: 1 -> 8; matrix products, arithmetic and copies ran while one was open for 18% -> 0% of each run, Pallas kernels for 0% -> 17%
where the time goes in v1:
time: 81.1 us; the launch traced here: 80.9 us
  waiting for transfers between devices  37.1 us (46%)
  starting transfers between devices  24.5 us (30%)
  Pallas kernels  15.1 us (19%)
  local copies, waits for them, and re-layouts  3.38 us (4%)
    ppermute x18, waiting for transfers between devices, xor_permute(): return lax.ppermute(x, axis, [(i, i ^ offset) for i in range(n)])  37.1 us
    ppermute x18, starting transfers between devices, xor_permute(): return lax.ppermute(x, axis, [(i, i ^ offset) for i in range(n)])  24.5 us
    pallas_call x6, Pallas kernels, call(): pl.pallas_call(kernel, out_shape=outs, in_specs=[far if i in hbm else vme...  15.1 us
    unnamed x9, local copies, waits for them, and re-layouts  3.32 us
  transfers between devices with their start and end apart: 18, of which 8 were waited for; matrix products, arithmetic and copies ran while one was open for 0% of the time, Pallas kernels for 17%

profile of v1, /device:TPU:0, one launch (start us, length us, event | category | flops | bytes accessed | tf_op | source)
XLA Modules:
  0.0 80.9 jit_solution(6398346512649809848)
XLA Ops:
  0.6 4.1 %collective-permute-start.11 = (bf16[64,1024]{1,0:T(8,128)(2,1)}, bf16[64,1024]{1,0:T(8,128)(2,1)S(1)}, u32[]{:S(2)}, u32[]{:S(2)}) collective-permute-start(bf16[64,1024]{1,0:T(8,128)(2,1)} %bitcast.6), channel_id=1, source_target_pairs={{0,16},{4,20},{8,24},{12,28},{16,0},{20,4},{24,8},{28,12},{1,17},{... | collective-permute-start | bytes 393224 | tf_op jit(solution)/shard_map/ppermute | solution.py:89
  4.8 0.0 copy-start
  4.8 1.0 %copy-done = bf16[1,256,1024]{2,1,0:T(8,128)(2,1)S(1)} copy-done((bf16[1,256,1024]{2,1,0:T(8,128)(2,1)S(1)}, bf16[1,256,1024]{2,1,0:T(8,128)(2,1)}, u32[]{:S(2)}) %copy-start) | copy-done | bytes 524312
  5.8 0.0 copy-start.1
  5.8 0.9 %copy-done.1 = bf16[1,64,1024]{2,1,0:T(8,128)(2,1)S(1)} copy-done((bf16[1,64,1024]{2,1,0:T(8,128)(2,1)S(1)}, bf16[1,64,1024]{2,1,0:T(8,128)(2,1)}, u32[]{:S(2)}) %copy-start.1) | copy-done | bytes 131096
  6.7 0.7 copy-done.2
  7.4 0.7 copy-done.3
  8.1 1.1 %shard_map.84 = (s32[1,1024]{1,0:T(1,128)S(1)}, bf16[256,1024]{1,0:T(8,128)(2,1)S(1)}, bf16[64,1024]{1,0:T(8,128)(2,1)S(1)}, bf16[1024]{0:T(1024)(128)(2,1)S(1)}...) custom-call(s32[1,1024]{1,0:T(1,128)S(1)} %copy-done.2, ...), custom_call_target="tpu_custom_call" | custom-call | flops 150994944 | bytes 1048576 | tf_op jit(solution)/shard_map/pallas_call | solution.py:286
  9.2 2.1 %collective-permute-done.11 = bf16[64,1024]{1,0:T(8,128)(2,1)S(1)} collective-permute-done((bf16[64,1024]{1,0:T(8,128)(2,1)}, bf16[64,1024]{1,0:T(8,128)(2,1)S(1)}, u32[]{:S(2)}, u32[]{:S(2)}) %collective-permute-start.11) | collective-permute-done | bytes 131104 | tf_op jit(solution)/shard_map/ppermute | solution.py:89
  11.3 0.9 %collective-permute-start.12 = (bf16[128,1024]{1,0:T(8,128)(2,1)S(1)}, bf16[128,1024]{1,0:T(8,128)(2,1)S(1)}, u32[]{:S(2)}, u32[]{:S(2)}) collective-permute-start(bf16[128,1024]{1,0:T(8,128)(2,1)S(1)} %pad_maximum_fusion), channel_id=1, source_target_pairs={{0,8},{4,12},{8,0},{12,4},{16,24},{20,28},{24,16},{28,20},{1,9},{5... | collective-permute-start | bytes 786440 | tf_op jit(solution)/shard_map/ppermute | solution.py:89
  12.2 6.6 %collective-permute-done.12 = bf16[128,1024]{1,0:T(8,128)(2,1)S(1)} collective-permute-done((bf16[128,1024]{1,0:T(8,128)(2,1)S(1)}, bf16[128,1024]{1,0:T(8,128)(2,1)S(1)}, u32[]{:S(2)}, u32[]{:S(2)}) %collective-permute-start.12) | collective-permute-done | bytes 262176 | tf_op jit(solution)/shard_map/ppermute | solution.py:89
  18.9 1.4 %collective-permute-start.14 = (bf16[192,1024]{1,0:T(8,128)(2,1)S(1)}, bf16[192,1024]{1,0:T(8,128)(2,1)S(1)}, u32[]{:S(2)}, u32[]{:S(2)}) collective-permute-start(bf16[192,1024]{1,0:T(8,128)(2,1)S(1)} %constant_dynamic-update-slice_fusion.e0), channel_id=1, source_target_pairs={{0,2},{1,3},{2,0},{3,1},{4,6},{5,7},{6,4},{7,5},{8,10},{9,11},{10,... | collective-permute-start | bytes 1179656 | tf_op jit(solution)/shard_map/ppermute | solution.py:89
  20.3 1.5 %collective-permute-start.13 = (bf16[192,1024]{1,0:T(8,128)(2,1)S(1)}, bf16[192,1024]{1,0:T(8,128)(2,1)S(1)}, u32[]{:S(2)}, u32[]{:S(2)}) collective-permute-start(bf16[192,1024]{1,0:T(8,128)(2,1)S(1)} %constant_dynamic-update-slice_fusion.e0), channel_id=1, source_target_pairs={{0,1},{1,0},{2,3},{3,2},{4,5},{5,4},{6,7},{7,6},{8,9},{9,8},{10,11... | collective-permute-start | bytes 1179656 | tf_op jit(solution)/shard_map/ppermute | solution.py:89
  21.8 0.5 collective-permute-start.3
  22.3 0.7 collective-permute-start.4
  23.0 2.3 %collective-permute-start.7 = (bf16[64,1024]{1,0:T(8,128)(2,1)S(1)}, bf16[64,1024]{1,0:T(8,128)(2,1)S(1)}, u32[]{:S(2)}, u32[]{:S(2)}) collective-permute-start(bf16[64,1024]{1,0:T(8,128)(2,1)S(1)} %get-tuple-element.32), channel_id=1, source_target_pairs={{0,3},{1,2},{2,1},{3,0},{4,7},{5,6},{6,5},{7,4},{8,11},{9,10},{10,... | collective-permute-start | bytes 393224 | tf_op jit(solution)/shard_map/ppermute | solution.py:89
  25.3 12.3 %collective-permute-done.3.x1 = bf16[128,1024]{1,0:T(8,128)(2,1)S(1)} collective-permute-done((bf16[128,1024]{1,0:T(8,128)(2,1)S(1)}, bf16[128,1024]{1,0:T(8,128)(2,1)S(1)}, u32[]{:S(2)}, u32[]{:S(2)}) %collective-permute-start.3) | collective-permute-done | bytes 262176 | tf_op jit(solution)/shard_map/ppermute | solution.py:89
  37.6 0.0 collective-permute-start.5
  37.6 0.0 collective-permute-done.4.x2
  37.6 1.7 %collective-permute-start.6 = (bf16[32,1024]{1,0:T(8,128)(2,1)S(1)}, bf16[32,1024]{1,0:T(8,128)(2,1)S(1)}, u32[]{:S(2)}, u32[]{:S(2)}) collective-permute-start(bf16[32,1024]{1,0:T(8,128)(2,1)S(1)} %slice.17), channel_id=1, source_target_pairs={{0,1},{1,0},{2,3},{3,2},{4,5},{5,4},{6,7},{7,6},{8,9},{9,8},{10,11... | collective-permute-start | bytes 196616 | tf_op jit(solution)/shard_map/ppermute | solution.py:89
  39.3 0.0 collective-permute-done.14.ey
  39.3 0.5 collective-permute-start.16
  39.8 0.0 collective-permute-done.13.ex
  39.8 2.1 %collective-permute-start.15 = (bf16[96,1024]{1,0:T(8,128)(2,1)S(1)}, bf16[96,1024]{1,0:T(8,128)(2,1)S(1)}, u32[]{:S(2)}, u32[]{:S(2)}) collective-permute-start(bf16[96,1024]{1,0:T(8,128)(2,1)S(1)} %slice.18), channel_id=1, source_target_pairs={{0,2},{1,3},{2,0},{3,1},{4,6},{5,7},{6,4},{7,5},{8,10},{9,11},{10,... | collective-permute-start | bytes 589832 | tf_op jit(solution)/shard_map/ppermute | solution.py:89
  41.9 0.0 collective-permute-done.7.x3
  41.9 0.8 shard_map.87
  42.6 1.9 %collective-permute-start.8 = (bf16[256,256]{1,0:T(8,128)(2,1)S(1)}, bf16[256,256]{1,0:T(8,128)(2,1)S(1)}, u32[]{:S(2)}, u32[]{:S(2)}) collective-permute-start(bf16[256,256]{1,0:T(8,128)(2,1)S(1)} %get-tuple-element.34), channel_id=1, source_target_pairs={{0,8},{4,12},{8,0},{12,4},{16,24},{20,28},{24,16},{28,20},{1,9},{5... | collective-permute-start | bytes 393224 | tf_op jit(solution)/shard_map/ppermute | solution.py:89
  44.6 0.0 collective-permute-done.5.cda
  44.6 3.3 %collective-permute-start.9 = (bf16[256,256]{1,0:T(8,128)(2,1)S(1)}, bf16[256,256]{1,0:T(8,128)(2,1)S(1)}, u32[]{:S(2)}, u32[]{:S(2)}) collective-permute-start(bf16[256,256]{1,0:T(8,128)(2,1)S(1)} %get-tuple-element.35), channel_id=1, source_target_pairs={{0,16},{4,20},{8,24},{12,28},{16,0},{20,4},{24,8},{28,12},{1,17},{... | collective-permute-start | bytes 393224 | tf_op jit(solution)/shard_map/ppermute | solution.py:89
  47.8 0.0 collective-permute-done.6.cdb
  47.8 0.0 collective-permute-start.10
  47.8 1.2 %collective-permute-done.8.m1 = bf16[256,256]{1,0:T(8,128)(2,1)S(1)} collective-permute-done((bf16[256,256]{1,0:T(8,128)(2,1)S(1)}, bf16[256,256]{1,0:T(8,128)(2,1)S(1)}, u32[]{:S(2)}, u32[]{:S(2)}) %collective-permute-start.8) | collective-permute-done | bytes 131104 | tf_op jit(solution)/shard_map/ppermute | solution.py:89
  49.1 3.1 %collective-permute-done.9.m2 = bf16[256,256]{1,0:T(8,128)(2,1)S(1)} collective-permute-done((bf16[256,256]{1,0:T(8,128)(2,1)S(1)}, bf16[256,256]{1,0:T(8,128)(2,1)S(1)}, u32[]{:S(2)}, u32[]{:S(2)}) %collective-permute-start.9) | collective-permute-done | bytes 131104 | tf_op jit(solution)/shard_map/ppermute | solution.py:89
  52.2 2.5 %collective-permute-done.10.m3 = bf16[256,256]{1,0:T(8,128)(2,1)S(1)} collective-permute-done((bf16[256,256]{1,0:T(8,128)(2,1)S(1)}, bf16[256,256]{1,0:T(8,128)(2,1)S(1)}, u32[]{:S(2)}, u32[]{:S(2)}) %collective-permute-start.10) | collective-permute-done | bytes 131104 | tf_op jit(solution)/shard_map/ppermute | solution.py:89
  54.7 0.0 collective-permute-done.16.edb
  54.7 0.0 collective-permute-done.15.eda
  54.7 0.8 %shard_map.88 = (f32[128,1024]{1,0:T(8,128)S(1)}, f32[8,1024]{1,0:T(8,128)S(1)}, f32[136,1024]{1,0:T(8,128)S(1)}) custom-call(bf16[256,256]{1,0:T(8,128)(2,1)S(1)} %get-tuple-element.33.m0, bf16[256,256]{1,0:T(8,128)(2,1)S(1)} %collective-permute-done.8.m1, bf16[256,256]{1,0:T(8,128)(2,1)S(1)} %collective-permute-done.9.m2, ...), custom_call_target="tpu_custom_call" | custom-call | flops 536870912 | bytes 2097152 | tf_op jit(solution)/shard_map/pallas_call | solution.py:286
  55.6 0.1 collective-permute-start.17
  55.7 1.6 %collective-permute-start = (bf16[96,1024]{1,0:T(8,128)(2,1)S(1)}, bf16[96,1024]{1,0:T(8,128)(2,1)S(1)}, u32[]{:S(2)}, u32[]{:S(2)}) collective-permute-start(bf16[96,1024]{1,0:T(8,128)(2,1)S(1)} %get-tuple-element.26), channel_id=1, source_target_pairs={{0,1},{1,0},{2,3},{3,2},{4,5},{5,4},{6,7},{7,6},{8,9},{9,8},{10,11... | collective-permute-start | bytes 589832 | tf_op jit(solution)/shard_map/ppermute | solution.py:89
  57.2 0.0 collective-permute-start.1
  57.2 2.0 %collective-permute-start.2 = (bf16[96,1024]{1,0:T(8,128)(2,1)S(1)}, bf16[96,1024]{1,0:T(8,128)(2,1)S(1)}, u32[]{:S(2)}, u32[]{:S(2)}) collective-permute-start(bf16[96,1024]{1,0:T(8,128)(2,1)S(1)} %get-tuple-element.28), channel_id=1, source_target_pairs={{0,3},{1,2},{2,1},{3,0},{4,7},{5,6},{6,5},{7,4},{8,11},{9,10},{10,... | collective-permute-start | bytes 589832 | tf_op jit(solution)/shard_map/ppermute | solution.py:89
  59.2 4.3 %collective-permute-done.p1 = bf16[96,1024]{1,0:T(8,128)(2,1)S(1)} collective-permute-done((bf16[96,1024]{1,0:T(8,128)(2,1)S(1)}, bf16[96,1024]{1,0:T(8,128)(2,1)S(1)}, u32[]{:S(2)}, u32[]{:S(2)}) %collective-permute-start) | collective-permute-done | bytes 196640 | tf_op jit(solution)/shard_map/ppermute | solution.py:89
  63.5 4.9 %collective-permute-done.1.p2 = bf16[96,1024]{1,0:T(8,128)(2,1)S(1)} collective-permute-done((bf16[96,1024]{1,0:T(8,128)(2,1)S(1)}, bf16[96,1024]{1,0:T(8,128)(2,1)S(1)}, u32[]{:S(2)}, u32[]{:S(2)}) %collective-permute-start.1) | collective-permute-done | bytes 196640 | tf_op jit(solution)/shard_map/ppermute | solution.py:89
  68.4 0.0 collective-permute-done.2.p3
  68.4 5.0 %shard_map.85 = bf16[64,1024]{1,0:T(8,128)(2,1)} custom-call(s32[1,1024]{1,0:T(1,128)S(1)} %get-tuple-element.23.order_ref, bf16[1024]{0:T(1024)(128)(2,1)S(1)} %get-tuple-element.24.bias_ref, bf16[256,1024]{1,0:T(8,128)(2,1)S(1)} %get-tuple-element.25.t_ref, bf16[96,1024]{1,0:T(8,128)(2,1)S(1)} %collective-permute-done.p1, ...), custom_call_target="tpu_custom_call" | custom-call | flops 1073741824 | bytes 8388608 | tf_op jit(solution)/shard_map/pallas_call | solution.py:286
  73.4 6.5 %shard_map.86 = bf16[256,1024]{1,0:T(8,128)(2,1)} custom-call(s32[1,1024]{1,0:T(1,128)S(1)} %get-tuple-element.23.order_ref, bf16[64,1024]{1,0:T(8,128)(2,1)S(1)} %get-tuple-element.29.c0, bf16[128,1024]{1,0:T(8,128)(2,1)S(1)} %collective-permute-done.3.x1, bf16[128,1024]{1,0:T(8,128)(2,1)S(1)} %collective-permute-done.4.x2, ...), custom_call_target="tpu_custom_call" | custom-call | flops 2684354560 | bytes 8388608 | tf_op jit(solution)/shard_map/pallas_call | solution.py:286
  80.0 0.0 collective-permute-done.17.taken
  80.0 0.9 %shard_map.89 = (f32[128,1024]{1,0:T(8,128)}, f32[1,1024]{1,0:T(1,128)}) custom-call(f32[128,1024]{1,0:T(8,128)S(1)} %get-tuple-element.37.keep, f32[8,1024]{1,0:T(8,128)S(1)} %get-tuple-element.38.keep_bias, f32[136,1024]{1,0:T(8,128)S(1)} %collective-permute-done.17.taken), custom_call_target="tpu_custom_call" | custom-call | flops 131072 | bytes 1572864 | tf_op jit(solution)/shard_map/pallas_call | solution.py:286
  (9 shorter events, 0.1 us)
Async XLA Ops:
  0.6 10.6 %collective-permute-start.11 = (bf16[64,1024]{1,0:T(8,128)(2,1)}, bf16[64,1024]{1,0:T(8,128)(2,1)S(1)}, u32[]{:S(2)}, u32[]{:S(2)}) collective-permute-start(bf16[64,1024]{1,0:T(8,128)(2,1)} %bitcast.6), channel_id=1, source_target_pairs={{0,16},{4,20},{8,24},{12,28},{16,0},{20,4},{24,8},{28,12},{1,17},{... | collective-permute-start | bytes 393224 | tf_op jit(solution)/shard_map/ppermute | solution.py:89
  4.8 1.0 %copy-start = (bf16[1,256,1024]{2,1,0:T(8,128)(2,1)S(1)}, bf16[1,256,1024]{2,1,0:T(8,128)(2,1)}, u32[]{:S(2)}) copy-start(bf16[1,256,1024]{2,1,0:T(8,128)(2,1)} %param.5) | copy-start | bytes 1572868
  5.8 0.9 %copy-start.1 = (bf16[1,64,1024]{2,1,0:T(8,128)(2,1)S(1)}, bf16[1,64,1024]{2,1,0:T(8,128)(2,1)}, u32[]{:S(2)}) copy-start(bf16[1,64,1024]{2,1,0:T(8,128)(2,1)} %param.9) | copy-start | bytes 393220
  6.7 0.7 copy-start.2
  7.4 0.7 copy-start.3
  11.3 7.5 %collective-permute-start.12 = (bf16[128,1024]{1,0:T(8,128)(2,1)S(1)}, bf16[128,1024]{1,0:T(8,128)(2,1)S(1)}, u32[]{:S(2)}, u32[]{:S(2)}) collective-permute-start(bf16[128,1024]{1,0:T(8,128)(2,1)S(1)} %pad_maximum_fusion), channel_id=1, source_target_pairs={{0,8},{4,12},{8,0},{12,4},{16,24},{20,28},{24,16},{28,20},{1,9},{5... | collective-permute-start | bytes 786440 | tf_op jit(solution)/shard_map/ppermute | solution.py:89
  18.9 20.4 %collective-permute-start.14 = (bf16[192,1024]{1,0:T(8,128)(2,1)S(1)}, bf16[192,1024]{1,0:T(8,128)(2,1)S(1)}, u32[]{:S(2)}, u32[]{:S(2)}) collective-permute-start(bf16[192,1024]{1,0:T(8,128)(2,1)S(1)} %constant_dynamic-update-slice_fusion.e0), channel_id=1, source_target_pairs={{0,2},{1,3},{2,0},{3,1},{4,6},{5,7},{6,4},{7,5},{8,10},{9,11},{10,... | collective-permute-start | bytes 1179656 | tf_op jit(solution)/shard_map/ppermute | solution.py:89
  20.3 19.5 %collective-permute-start.13 = (bf16[192,1024]{1,0:T(8,128)(2,1)S(1)}, bf16[192,1024]{1,0:T(8,128)(2,1)S(1)}, u32[]{:S(2)}, u32[]{:S(2)}) collective-permute-start(bf16[192,1024]{1,0:T(8,128)(2,1)S(1)} %constant_dynamic-update-slice_fusion.e0), channel_id=1, source_target_pairs={{0,1},{1,0},{2,3},{3,2},{4,5},{5,4},{6,7},{7,6},{8,9},{9,8},{10,11... | collective-permute-start | bytes 1179656 | tf_op jit(solution)/shard_map/ppermute | solution.py:89
  21.8 15.8 %collective-permute-start.3 = (bf16[128,1024]{1,0:T(8,128)(2,1)S(1)}, bf16[128,1024]{1,0:T(8,128)(2,1)S(1)}, u32[]{:S(2)}, u32[]{:S(2)}) collective-permute-start(bf16[128,1024]{1,0:T(8,128)(2,1)S(1)} %get-tuple-element.30), channel_id=1, source_target_pairs={{0,1},{1,0},{2,3},{3,2},{4,5},{5,4},{6,7},{7,6},{8,9},{9,8},{10,11... | collective-permute-start | bytes 786440 | tf_op jit(solution)/shard_map/ppermute | solution.py:89
  22.3 15.3 %collective-permute-start.4 = (bf16[128,1024]{1,0:T(8,128)(2,1)S(1)}, bf16[128,1024]{1,0:T(8,128)(2,1)S(1)}, u32[]{:S(2)}, u32[]{:S(2)}) collective-permute-start(bf16[128,1024]{1,0:T(8,128)(2,1)S(1)} %get-tuple-element.31), channel_id=1, source_target_pairs={{0,2},{1,3},{2,0},{3,1},{4,6},{5,7},{6,4},{7,5},{8,10},{9,11},{10,... | collective-permute-start | bytes 786440 | tf_op jit(solution)/shard_map/ppermute | solution.py:89
  23.0 18.9 %collective-permute-start.7 = (bf16[64,1024]{1,0:T(8,128)(2,1)S(1)}, bf16[64,1024]{1,0:T(8,128)(2,1)S(1)}, u32[]{:S(2)}, u32[]{:S(2)}) collective-permute-start(bf16[64,1024]{1,0:T(8,128)(2,1)S(1)} %get-tuple-element.32), channel_id=1, source_target_pairs={{0,3},{1,2},{2,1},{3,0},{4,7},{5,6},{6,5},{7,4},{8,11},{9,10},{10,... | collective-permute-start | bytes 393224 | tf_op jit(solution)/shard_map/ppermute | solution.py:89
  37.6 7.0 %collective-permute-start.5 = (bf16[32,1024]{1,0:T(8,128)(2,1)S(1)}, bf16[32,1024]{1,0:T(8,128)(2,1)S(1)}, u32[]{:S(2)}, u32[]{:S(2)}) collective-permute-start(bf16[32,1024]{1,0:T(8,128)(2,1)S(1)} %slice.16), channel_id=1, source_target_pairs={{0,2},{1,3},{2,0},{3,1},{4,6},{5,7},{6,4},{7,5},{8,10},{9,11},{10,... | collective-permute-start | bytes 196616 | tf_op jit(solution)/shard_map/ppermute | solution.py:89
  37.6 10.2 %collective-permute-start.6 = (bf16[32,1024]{1,0:T(8,128)(2,1)S(1)}, bf16[32,1024]{1,0:T(8,128)(2,1)S(1)}, u32[]{:S(2)}, u32[]{:S(2)}) collective-permute-start(bf16[32,1024]{1,0:T(8,128)(2,1)S(1)} %slice.17), channel_id=1, source_target_pairs={{0,1},{1,0},{2,3},{3,2},{4,5},{5,4},{6,7},{7,6},{8,9},{9,8},{10,11... | collective-permute-start | bytes 196616 | tf_op jit(solution)/shard_map/ppermute | solution.py:89
  39.3 15.4 %collective-permute-start.16 = (bf16[96,1024]{1,0:T(8,128)(2,1)S(1)}, bf16[96,1024]{1,0:T(8,128)(2,1)S(1)}, u32[]{:S(2)}, u32[]{:S(2)}) collective-permute-start(bf16[96,1024]{1,0:T(8,128)(2,1)S(1)} %slice.19), channel_id=1, source_target_pairs={{0,1},{1,0},{2,3},{3,2},{4,5},{5,4},{6,7},{7,6},{8,9},{9,8},{10,11... | collective-permute-start | bytes 589832 | tf_op jit(solution)/shard_map/ppermute | solution.py:89
  39.8 14.9 %collective-permute-start.15 = (bf16[96,1024]{1,0:T(8,128)(2,1)S(1)}, bf16[96,1024]{1,0:T(8,128)(2,1)S(1)}, u32[]{:S(2)}, u32[]{:S(2)}) collective-permute-start(bf16[96,1024]{1,0:T(8,128)(2,1)S(1)} %slice.18), channel_id=1, source_target_pairs={{0,2},{1,3},{2,0},{3,1},{4,6},{5,7},{6,4},{7,5},{8,10},{9,11},{10,... | collective-permute-start | bytes 589832 | tf_op jit(solution)/shard_map/ppermute | solution.py:89
  42.6 6.4 %collective-permute-start.8 = (bf16[256,256]{1,0:T(8,128)(2,1)S(1)}, bf16[256,256]{1,0:T(8,128)(2,1)S(1)}, u32[]{:S(2)}, u32[]{:S(2)}) collective-permute-start(bf16[256,256]{1,0:T(8,128)(2,1)S(1)} %get-tuple-element.34), channel_id=1, source_target_pairs={{0,8},{4,12},{8,0},{12,4},{16,24},{20,28},{24,16},{28,20},{1,9},{5... | collective-permute-start | bytes 393224 | tf_op jit(solution)/shard_map/ppermute | solution.py:89
  44.6 7.6 %collective-permute-start.9 = (bf16[256,256]{1,0:T(8,128)(2,1)S(1)}, bf16[256,256]{1,0:T(8,128)(2,1)S(1)}, u32[]{:S(2)}, u32[]{:S(2)}) collective-permute-start(bf16[256,256]{1,0:T(8,128)(2,1)S(1)} %get-tuple-element.35), channel_id=1, source_target_pairs={{0,16},{4,20},{8,24},{12,28},{16,0},{20,4},{24,8},{28,12},{1,17},{... | collective-permute-start | bytes 393224 | tf_op jit(solution)/shard_map/ppermute | solution.py:89
  47.8 6.9 %collective-permute-start.10 = (bf16[256,256]{1,0:T(8,128)(2,1)S(1)}, bf16[256,256]{1,0:T(8,128)(2,1)S(1)}, u32[]{:S(2)}, u32[]{:S(2)}) collective-permute-start(bf16[256,256]{1,0:T(8,128)(2,1)S(1)} %get-tuple-element.36), channel_id=1, source_target_pairs={{0,24},{4,28},{8,16},{12,20},{16,8},{20,12},{24,0},{28,4},{1,25},{... | collective-permute-start | bytes 393224 | tf_op jit(solution)/shard_map/ppermute | solution.py:89
  55.6 24.4 %collective-permute-start.17 = (f32[136,1024]{1,0:T(8,128)S(1)}, f32[136,1024]{1,0:T(8,128)S(1)}, u32[]{:S(2)}, u32[]{:S(2)}) collective-permute-start(f32[136,1024]{1,0:T(8,128)S(1)} %get-tuple-element.39), channel_id=1, source_target_pairs={{0,4},{4,0},{8,12},{12,8},{16,20},{20,16},{24,28},{28,24},{1,5},{5... | collective-permute-start | bytes 1671176 | tf_op jit(solution)/shard_map/ppermute | solution.py:89
  55.7 7.8 %collective-permute-start = (bf16[96,1024]{1,0:T(8,128)(2,1)S(1)}, bf16[96,1024]{1,0:T(8,128)(2,1)S(1)}, u32[]{:S(2)}, u32[]{:S(2)}) collective-permute-start(bf16[96,1024]{1,0:T(8,128)(2,1)S(1)} %get-tuple-element.26), channel_id=1, source_target_pairs={{0,1},{1,0},{2,3},{3,2},{4,5},{5,4},{6,7},{7,6},{8,9},{9,8},{10,11... | collective-permute-start | bytes 589832 | tf_op jit(solution)/shard_map/ppermute | solution.py:89
  57.2 11.2 %collective-permute-start.1 = (bf16[96,1024]{1,0:T(8,128)(2,1)S(1)}, bf16[96,1024]{1,0:T(8,128)(2,1)S(1)}, u32[]{:S(2)}, u32[]{:S(2)}) collective-permute-start(bf16[96,1024]{1,0:T(8,128)(2,1)S(1)} %get-tuple-element.27), channel_id=1, source_target_pairs={{0,2},{1,3},{2,0},{3,1},{4,6},{5,7},{6,4},{7,5},{8,10},{9,11},{10,... | collective-permute-start | bytes 589832 | tf_op jit(solution)/shard_map/ppermute | solution.py:89
  57.2 11.1 %collective-permute-start.2 = (bf16[96,1024]{1,0:T(8,128)(2,1)S(1)}, bf16[96,1024]{1,0:T(8,128)(2,1)S(1)}, u32[]{:S(2)}, u32[]{:S(2)}) collective-permute-start(bf16[96,1024]{1,0:T(8,128)(2,1)S(1)} %get-tuple-element.28), channel_id=1, source_target_pairs={{0,3},{1,2},{2,1},{3,0},{4,7},{5,6},{6,5},{7,4},{8,11},{9,10},{10,... | collective-permute-start | bytes 589832 | tf_op jit(solution)/shard_map/ppermute | solution.py:89

commit v2 on v1

v2 whole, which is shorter than its diff:
```python
import functools
import math

import jax
import jax.numpy as jnp
from jax import lax
from jax.experimental import pallas as pl
from jax.experimental.pallas import tpu as pltpu
from jax.sharding import PartitionSpec as P


COLS = 128
MERGE = 4
SPANS = 4
LANES = 128
MAIN_LIMIT = 44


def general_body(tokens, scan_order, w_merge, bias, cotangent):
    spans = lax.axis_size("span")
    views = lax.axis_size("view")
    span_index = lax.axis_index("span")
    tok_dev = tokens.shape[1]
    width = tokens.shape[2]
    capacity = 3 * (tok_dev // spans) // 2
    rows_dev = tok_dev // COLS
    order_all = scan_order[0].reshape(spans, tok_dev)
    owners = order_all // tok_dev
    owner_hot = (owners[:, :, None] == jnp.arange(spans, dtype=jnp.int32)[None, None, :]).astype(
        jnp.int32
    )
    slot_rank = jnp.sum((jnp.cumsum(owner_hot, axis=1) - 1) * owner_hot, axis=2)
    dest_slots = owners * capacity + slot_rank
    my_slots = lax.dynamic_index_in_dim(dest_slots, span_index, 0, keepdims=False)
    outgoing = jnp.zeros((spans * capacity, width), jnp.bfloat16).at[my_slots].set(tokens[0])
    received = lax.all_to_all(
        outgoing.reshape(spans, capacity, width), "span", split_axis=0, concat_axis=0, tiled=True
    )
    arriving = owners == span_index
    source_slot = jnp.arange(spans, dtype=jnp.int32)[:, None] * capacity + slot_rank
    local_index = jnp.where(arriving, order_all - span_index * tok_dev, tok_dev)
    source_of = (
        jnp.zeros((tok_dev,), jnp.int32)
        .at[local_index.reshape(-1)]
        .set(source_slot.reshape(-1), mode="drop")
    )
    raster = received.reshape(spans * capacity, width)[source_of]
    merged = (
        raster.reshape(rows_dev // 2, 2, COLS // 2, 2, width)
        .transpose(0, 2, 1, 3, 4)
        .reshape(tok_dev // 4, 4 * width)
    )
    merged_out = (
        jnp.dot(merged, w_merge, preferred_element_type=jnp.float32) + bias.astype(jnp.float32)
    ).astype(jnp.bfloat16)
    grads = cotangent[0]
    grad_merged = lax.dot_general(
        grads, w_merge, (((1,), (1,)), ((), ())), preferred_element_type=jnp.float32
    ).astype(jnp.bfloat16)
    grad_raster = (
        grad_merged.reshape(rows_dev // 2, COLS // 2, 2, 2, width)
        .transpose(0, 2, 1, 3, 4)
        .reshape(tok_dev, width)
    )
    going_back = jnp.zeros((spans * capacity, width), jnp.bfloat16).at[source_of].set(grad_raster)
    returned = lax.all_to_all(
        going_back.reshape(spans, capacity, width), "span", split_axis=0, concat_axis=0, tiled=True
    )
    token_grad = returned.reshape(spans * capacity, width)[my_slots]
    kernel_rows = 4 * width
    merged_rows = merged.shape[0]
    group_rows = kernel_rows // (views * spans)
    regrouped = merged.reshape(merged_rows, views, spans, group_rows).transpose(0, 2, 1, 3)
    view_tokens = lax.all_to_all(regrouped, "span", split_axis=1, concat_axis=0, tiled=True)
    view_tokens = view_tokens.reshape(spans * merged_rows, views * group_rows)
    all_grads = lax.all_gather(grads, "span", axis=0, tiled=True)
    partial_sum = lax.dot_general(
        view_tokens, all_grads, (((0,), (0,)), ((), ())), preferred_element_type=jnp.float32
    )
    weight_sum = lax.psum_scatter(partial_sum, "view", scatter_dimension=0, tiled=True)
    bias_total = lax.psum(jnp.sum(grads.astype(jnp.float32), axis=0), ("view", "span"))
    grad_scale = 1.0 / math.sqrt(views * spans * (tok_dev // 4))
    return (merged_out[None], token_grad[None], weight_sum * grad_scale, bias_total * grad_scale)


def xor_permute(x, view_offset, span_offset):
    views, spans = lax.axis_size("view"), lax.axis_size("span")
    pairs = []
    for i in range(views * spans):
        view, span = divmod(i, spans)
        step = span_offset[view % 2] if span_offset else 0
        pairs.append((i, (view ^ view_offset) * spans + (span ^ step)))
    return lax.ppermute(x, ("view", "span"), pairs)


def raster_of(k, band, local, tok_dev):
    half = COLS // 2
    row = local // half
    col = local % half
    return band * tok_dev + (2 * row + k // 2) * COLS + 2 * col + k % 2


def order_row(order_ref, block, tok_dev):
    return order_ref[:, pl.ds(pl.multiple_of(block * tok_dev, LANES), tok_dev)]


def bf16_hot(mask):
    return jnp.where(mask, 1.0, 0.0).astype(jnp.bfloat16)


def rank_of(member):
    n = member.shape[1]
    upper = lax.broadcasted_iota(jnp.int32, (n, n), 0) <= lax.broadcasted_iota(jnp.int32, (n, n), 1)
    rows = jnp.broadcast_to(bf16_hot(member), (16, n))
    count = jnp.dot(rows, bf16_hot(upper), preferred_element_type=jnp.float32)
    return count[:1].astype(jnp.int32) - 1


def slot_hot(order, band, tok_dev, slots):
    member = (order // tok_dev) == band
    slot = lax.broadcasted_iota(jnp.int32, (slots, order.shape[1]), 0)
    return jnp.where(member & (rank_of(member) == slot), 1.0, 0.0).astype(jnp.bfloat16)


def band_offsets():
    core = lax.axis_index("view") % 2
    return (0, 1 + core, 2 - core, 3)


def band_of(block, s):
    offset = jnp.zeros_like(block)
    for j, o in enumerate(band_offsets()):
        offset = jnp.where(block == j, o, offset)
    return s ^ offset


def channel_starts(s, group):
    return [pl.multiple_of(s * group + c * SPANS * group, LANES) for c in range(2)]


def pack_kernel(order_ref, t_in, t_ref, q_first, q_second, p_first, p_second):
    tok_dev = t_in.shape[0]
    mrows = tok_dev // MERGE
    slots = p_second.shape[0] // 2
    group = LANES
    s = lax.axis_index("span")
    _, h, g, d = band_offsets()
    t_ref[...] = t_in[...]
    for o, q, first in ((h, q_first, 0), (d, q_first, mrows), (g, q_second, 0)):
        for c, start in enumerate(channel_starts(s ^ o, group)):
            for j in range(MERGE):
                column = (2 * j + c) * group
                q[first:first + mrows, column:column + group] = t_in[
                    j * mrows:(j + 1) * mrows, pl.ds(start, group)
                ]
    order = order_row(order_ref, s, tok_dev)
    for o, p, first in ((h, p_first, 0), (d, p_first, slots), (g, p_second, 0)):
        hot = slot_hot(order, s ^ o, tok_dev, slots)
        rows = jnp.dot(hot, t_in[...], preferred_element_type=jnp.float32)
        p[first:first + slots, :] = rows.astype(p.dtype)


def hold_kernel(c_ref, c_out):
    c_out[:c_ref.shape[0], :] = c_ref[...]


def stage_kernel(first, w_hbm, *refs):
    *outs, sems = refs
    width = outs[0].shape[0]
    copies = []
    for i, out in enumerate(outs):
        rows = pl.ds((first + i) * width, width)
        copies.append(pltpu.make_async_copy(w_hbm.at[rows, :], out, sems.at[i]))
        copies[-1].start()
    for copy in copies:
        copy.wait()


def select_kernel(order_ref, t_ref, q_near, q_far, m0, m1, m2, m3):
    tok_dev = t_ref.shape[0]
    mrows = tok_dev // MERGE
    group = LANES
    s = lax.axis_index("span")
    z = lax.axis_index("view") // 2
    order = jnp.concatenate([order_row(order_ref, s ^ o, tok_dev) for o in band_offsets()], axis=1)
    mine = [t_ref[:, pl.ds(start, group)] for start in channel_starts(s, group)]
    parts = [jnp.concatenate(mine, axis=1)]
    for q, first in ((q_near, 0), (q_far, 0), (q_far, mrows)):
        parts += [
            q[first:first + mrows, 2 * j * group:2 * (j + 1) * group] for j in range(MERGE)
        ]
    slab = jnp.concatenate(parts, axis=0)
    target = lax.broadcasted_iota(jnp.int32, (tok_dev, 1), 0)
    band = band_of(target // mrows, s)
    local = target % mrows
    for dz, out in enumerate((m0, m1, m2, m3)):
        raster = raster_of(z ^ dz, band, local, tok_dev)
        hot = bf16_hot(raster == order)
        out[...] = jnp.dot(hot, slab, preferred_element_type=jnp.float32).astype(out.dtype)


def forward_kernel(order_ref, bias_ref, t_ref, p_near, p_far, w0, w1, w2, w3, out):
    tok_dev = t_ref.shape[0]
    mrows = tok_dev // MERGE
    slots = p_far.shape[0] // 2
    s = lax.axis_index("span")
    _, h, g, d = band_offsets()
    f32 = jnp.float32
    local = lax.broadcasted_iota(jnp.int32, (tok_dev, 1), 0)
    raster = raster_of(local // mrows, s, local % mrows, tok_dev)
    mine_order = order_row(order_ref, s, tok_dev)
    mine = jnp.dot(bf16_hot(raster == mine_order), t_ref[...], preferred_element_type=f32)
    key = raster - s * tok_dev + 1
    for o, p, first in ((h, p_near, 0), (g, p_far, 0), (d, p_far, slots)):
        order = order_row(order_ref, s ^ o, tok_dev)
        held = slot_hot(order, s, tok_dev, slots)
        place = jnp.where(order // tok_dev == s, order - s * tok_dev + 1, 0)
        place = jnp.broadcast_to(place, (16, tok_dev)).astype(f32).astype(jnp.bfloat16)
        held = lax.dot_general(place, held, (((1,), (1,)), ((), ())), preferred_element_type=f32)
        hot = bf16_hot(key == held[:1].astype(jnp.int32))
        mine += jnp.dot(hot, p[first:first + slots, :], preferred_element_type=f32)
    mine = mine.astype(jnp.bfloat16)
    acc = bias_ref[...].astype(f32).reshape(1, -1)
    for k, w in enumerate((w0, w1, w2, w3)):
        rows = mine[k * mrows:(k + 1) * mrows, :]
        acc = acc + jnp.dot(rows, w[...], preferred_element_type=f32)
    out[...] = acc.astype(out.dtype)


def backward_kernel(order_ref, near, far, w0, w1, w2, w3, tgrad):
    mrows = near.shape[0] // 2
    tok_dev = MERGE * mrows
    s = lax.axis_index("span")
    f32 = jnp.float32
    grads = jnp.concatenate([near[...], far[...]], axis=0)
    local = lax.broadcasted_iota(jnp.int32, (tok_dev, 1), 0)
    band = band_of(local // mrows, s)
    order = order_row(order_ref, s, tok_dev)
    hots = []
    rasters = []
    for k, w in enumerate((w0, w1, w2, w3)):
        hots.append(bf16_hot(raster_of(k, band, local % mrows, tok_dev) == order))
        rasters.append(
            lax.dot_general(
                grads, w[...], (((1,), (1,)), ((), ())), preferred_element_type=f32
            ).astype(jnp.bfloat16)
        )
    tgrad[...] = lax.dot_general(
        jnp.concatenate(hots, axis=0),
        jnp.concatenate(rasters, axis=0),
        (((0,), (0,)), ((), ())),
        preferred_element_type=f32,
    ).astype(tgrad.dtype)


def weight_kernel(m0, m1, m2, m3, cnear, cfar, e0, e1, e2, e3, keep, keep_bias, give):
    mrows = cnear.shape[0] // 2
    core = lax.axis_index("view") % 2
    f32 = jnp.float32

    def stacked(j):
        return jnp.concatenate(
            [m[j * mrows:(j + 1) * mrows, :] for m in (m0, m1, m2, m3)], axis=0
        )

    lhs = jnp.concatenate([stacked(j) for j in range(SPANS)], axis=0)
    blocks = []
    for c, pair in ((cnear, (e0, e1)), (cfar, (e2, e3))):
        for j, e in enumerate(pair):
            blocks += [c[j * mrows:(j + 1) * mrows, :], e[...]]
    rhs = jnp.concatenate(blocks, axis=0)
    group = lhs.shape[1] // 2
    total = lax.dot_general(lhs, rhs, (((0,), (0,)), ((), ())), preferred_element_type=f32)
    low, high = total[:group], total[group:]
    mine = core == 0
    keep[...] = jnp.where(mine, low, high)
    give[:group, :] = jnp.where(mine, high, low)
    pieces = rhs.astype(f32).reshape(SPANS, MERGE, mrows, rhs.shape[1])

    def block_sum(b):
        return (b[0] + b[1]) + (b[2] + b[3])

    sums = [block_sum(pieces[j]) for j in range(SPANS)]
    tree = (sums[0] + sums[1]) + (sums[2] + sums[3])
    bias = jnp.broadcast_to(jnp.sum(tree, axis=0, keepdims=True), keep_bias.shape)
    keep_bias[...] = bias
    give[group:, :] = bias


def finish_kernel(scale, keep, keep_bias, taken, weight_grad, bias_grad):
    group = keep.shape[0]
    weight_grad[...] = (keep[...] + taken[:group, :]) * scale
    bias_grad[...] = (keep_bias[:1, :] + taken[group:group + 1, :]) * scale


def shape(rows, cols, dtype=jnp.bfloat16):
    return jax.ShapeDtypeStruct((rows, cols), dtype)


def call(kernel, args, outs, cost, hbm=(), scratch=(), limit=32):
    vmem = pl.BlockSpec(memory_space=pltpu.VMEM)
    far = pl.BlockSpec(memory_space=pltpu.HBM)
    return pl.pallas_call(
        kernel,
        out_shape=outs,
        in_specs=[far if i in hbm else vmem for i in range(len(args))],
        out_specs=[vmem] * len(outs),
        scratch_shapes=scratch,
        cost_estimate=cost,
        compiler_params=pltpu.CompilerParams(vmem_limit_bytes=int(limit * 1024 * 1024)),
    )(*args)


def cost_of(flops, moved):
    return pl.CostEstimate(flops=flops, bytes_accessed=moved, transcendentals=0)


def join_rows(buffer, tail):
    return lax.dynamic_update_slice(buffer, tail, (buffer.shape[0] - tail.shape[0], 0))


def quad_steps(tokens, scan_order, w_merge, bias, cotangent):
    spans = lax.axis_size("span")
    views = lax.axis_size("view")
    tok_dev = tokens.shape[1]
    width = tokens.shape[2]
    mrows = tok_dev // MERGE
    group = MERGE * width // (views * spans)
    f32 = jnp.float32
    t0 = tokens[0]
    c0 = cotangent[0]

    def hop(x, view_offset=0, span_offset=None):
        return xor_permute(x, view_offset, span_offset)

    first, second = (1, 2), (2, 1)
    capacity = 3 * (tok_dev // spans) // 2
    c1 = hop(c0, span_offset=first)
    zs = [hop(c0, view_offset=2 * dz) for dz in range(1, MERGE)]
    tv, q_first, q_second, p_first, p_second = call(
        pack_kernel,
        (scan_order, t0),
        [
            shape(tok_dev, width),
            shape(2 * mrows, width),
            shape(2 * mrows, width),
            shape(2 * capacity, width),
            shape(2 * capacity, width),
        ],
        cost_of(2 * 3 * capacity * tok_dev * width, 4 * tok_dev * width),
    )
    q_near = hop(q_first, span_offset=first)
    p_near = hop(p_first, span_offset=first)
    (c_half,) = call(
        hold_kernel, (c0,), [shape(2 * mrows, width)], cost_of(width, 4 * mrows * width)
    )
    q_far = hop(join_rows(q_second, q_near[mrows:]), span_offset=second)
    p_far = hop(join_rows(p_second, p_near[capacity:]), span_offset=second)
    cnear = join_rows(c_half, c1)
    cfar = hop(cnear, span_offset=second)
    extra = jnp.concatenate(zs, axis=0)
    e1 = hop(extra, span_offset=first)
    e2 = hop(extra, span_offset=second)
    e3 = hop(e1, span_offset=second)
    picks = call(
        select_kernel,
        (scan_order, tv, q_near, q_far),
        [shape(tok_dev, 2 * group)] * MERGE,
        cost_of(2 * spans * spans * tok_dev * tok_dev * 2 * group, 4 * tok_dev * width),
    )
    ms = [picks[0]] + [hop(picks[dz], view_offset=2 * dz) for dz in range(1, MERGE)]
    weights = []
    for first in range(0, MERGE, 2):
        weights += call(
            functools.partial(stage_kernel, first),
            (w_merge,),
            [shape(width, width)] * 2,
            cost_of(width, 4 * width * width),
            hbm=(0,),
            scratch=[pltpu.SemaphoreType.DMA((2,))],
            limit=MAIN_LIMIT,
        )
    (token_grad,) = call(
        backward_kernel,
        (scan_order, cnear, cfar, *weights),
        [shape(tok_dev, width)],
        cost_of(10 * tok_dev * width * width, 8 * width * width),
    )
    (merged_out,) = call(
        forward_kernel,
        (scan_order, bias, tv, p_near, p_far, *weights),
        [shape(mrows, width)],
        cost_of(4 * tok_dev * width * width, 8 * width * width),
    )
    keep, keep_bias, give = call(
        weight_kernel,
        (*ms, cnear, cfar, extra, e1, e2, e3),
        [shape(group, width, f32), shape(8, width, f32), shape(group + 8, width, f32)],
        cost_of(4 * spans * tok_dev * group * width, 8 * tok_dev * width),
    )
    taken = hop(give, view_offset=1)
    scale = 1.0 / math.sqrt(views * spans * mrows)
    weight_grad, bias_grad = call(
        functools.partial(finish_kernel, scale),
        (keep, keep_bias, taken),
        [shape(group, width, f32), shape(1, width, f32)],
        cost_of(group * width, 12 * group * width),
    )
    return merged_out[None], token_grad[None], weight_grad, bias_grad[0]


def body(tokens, scan_order, w_merge, bias, cotangent):
    spans = lax.axis_size("span")
    views = lax.axis_size("view")
    width = tokens.shape[2]
    group = MERGE * width // (views * spans)
    if spans == SPANS and views == 2 * MERGE and group == LANES:
        return quad_steps(tokens, scan_order, w_merge, bias, cotangent)
    return general_body(tokens, scan_order, w_merge, bias, cotangent)


def solution(mesh):
    in_specs = (P("view", "span", None), P("view", None), P(), P(), P("view", "span", None))
    out_specs = (P("view", "span", None), P("view", "span", None), P(("view", "span"), None), P())
    return jax.shard_map(body, mesh=mesh, in_specs=in_specs, out_specs=out_specs, check_vma=False)
```

time: 81.1 us -> 65.3 us (0.81)
  waiting for transfers between devices: 37.1 us -> 23.6 us
  starting transfers between devices: 24.5 us -> 22.9 us
    ppermute x18 -> x16, waiting for transfers between devices: 37.1 us -> 23.6 us  [xor_permute(): return lax.ppermute(x, ('view', 'span'), pairs)]
    ppermute x18 -> x16, starting transfers between devices: 24.5 us -> 22.9 us  [xor_permute(): return lax.ppermute(x, ('view', 'span'), pairs)]
    unnamed x9 -> x12, local copies, waits for them, and re-layouts: 3.32 us -> 2.7 us
    pallas_call x6 -> x9, Pallas kernels: 15.1 us -> 15.1 us  [call(): pl.pallas_call(kernel, out_shape=outs, in_specs=[far if i in hbm else vme...]
  transfers between devices with their start and end apart: 18 -> 16, of which waited for: 8 -> 5; matrix products, arithmetic and copies ran while one was open for 0% -> 0% of each run, Pallas kernels for 17% -> 22%
where the time goes in v2:
time: 65.3 us; the launch traced here: 65.1 us
  waiting for transfers between devices  23.6 us (36%)
  starting transfers between devices  22.9 us (35%)
  Pallas kernels  15.1 us (23%)
  local copies, waits for them, and re-layouts  2.74 us (4%)
  between operations  0.76 us (1%)
    ppermute x16, waiting for transfers between devices, xor_permute(): return lax.ppermute(x, ('view', 'span'), pairs)  23.6 us
    ppermute x16, starting transfers between devices, xor_permute(): return lax.ppermute(x, ('view', 'span'), pairs)  22.9 us
    pallas_call x9, Pallas kernels, call(): pl.pallas_call(kernel, out_shape=outs, in_specs=[far if i in hbm else vme...  15.1 us
    unnamed x12, local copies, waits for them, and re-layouts  2.7 us
  transfers between devices with their start and end apart: 16, of which 5 were waited for; matrix products, arithmetic and copies ran while one was open for 0% of the time, Pallas kernels for 22%

profile of v2, /device:TPU:0, one launch (start us, length us, event | category | flops | bytes accessed | tf_op | source)
XLA Modules:
  0.0 65.1 jit_solution(6001168402608040909)
XLA Ops:
  0.6 3.1 %collective-permute-start.9 = (bf16[64,1024]{1,0:T(8,128)(2,1)}, bf16[64,1024]{1,0:T(8,128)(2,1)S(1)}, u32[]{:S(2)}, u32[]{:S(2)}) collective-permute-start(bf16[64,1024]{1,0:T(8,128)(2,1)} %bitcast.5), channel_id=1, source_target_pairs={{0,8},{1,9},{2,10},{3,11},{4,12},{5,13},{6,14},{7,15},{8,0},{9,1},... | collective-permute-start | bytes 393224 | tf_op jit(solution)/shard_map/ppermute | solution.py:93
  3.7 2.6 %collective-permute-start.10 = (bf16[64,1024]{1,0:T(8,128)(2,1)}, bf16[64,1024]{1,0:T(8,128)(2,1)S(1)}, u32[]{:S(2)}, u32[]{:S(2)}) collective-permute-start(bf16[64,1024]{1,0:T(8,128)(2,1)} %bitcast.6), channel_id=1, source_target_pairs={{0,16},{1,17},{2,18},{3,19},{4,20},{5,21},{6,22},{7,23},{8,24},{9,... | collective-permute-start | bytes 393224 | tf_op jit(solution)/shard_map/ppermute | solution.py:93
  6.3 0.0 collective-permute-start.11
  6.3 0.0 copy-start.1
  6.3 0.7 %copy-done.1 = s32[1,1024]{1,0:T(1,128)S(1)} copy-done((s32[1,1024]{1,0:T(1,128)S(1)}, s32[1,1024]{1,0:T(1,128)}, u32[]{:S(2)}) %copy-start.1) | copy-done | bytes 4120
  7.0 1.0 %copy-done.4 = bf16[1,256,1024]{2,1,0:T(8,128)(2,1)S(1)} copy-done((bf16[1,256,1024]{2,1,0:T(8,128)(2,1)S(1)}, bf16[1,256,1024]{2,1,0:T(8,128)(2,1)}, u32[]{:S(2)}) %copy-start.4) | copy-done | bytes 524312
  8.1 0.8 %shard_map.84 = (bf16[256,1024]{1,0:T(8,128)(2,1)S(1)}, bf16[128,1024]{1,0:T(8,128)(2,1)S(1)}, bf16[128,1024]{1,0:T(8,128)(2,1)S(1)}, bf16[192,1024]{1,0:T(8,128)(2,1)S(1)}, bf16[192,1024]{1,0:T(8,128)(2,1)S(1)}) custom-call(s32[1,1024]{1,0:T(1,128)S(1)} %copy-done.1, bf16[256,1024]{1,0:T(8,128)(2,1)S(1)} %bitcast.10), custom_call_target="tpu_custom_call" | custom-call | flops 150994944 | bytes 1048576 | tf_op jit(solution)/shard_map/pallas_call | solution.py:303
  8.9 1.8 %collective-permute-start.4 = (bf16[128,1024]{1,0:T(8,128)(2,1)S(1)}, bf16[128,1024]{1,0:T(8,128)(2,1)S(1)}, u32[]{:S(2)}, u32[]{:S(2)}) collective-permute-start(bf16[128,1024]{1,0:T(8,128)(2,1)S(1)} %get-tuple-element.29), channel_id=1, source_target_pairs={{0,1},{1,0},{2,3},{3,2},{4,6},{5,7},{6,4},{7,5},{8,9},{9,8},{10,11... | collective-permute-start | bytes 786440 | tf_op jit(solution)/shard_map/ppermute | solution.py:93
  10.7 0.0 collective-permute-done.9
  10.7 6.1 %collective-permute-done.10 = bf16[64,1024]{1,0:T(8,128)(2,1)S(1)} collective-permute-done((bf16[64,1024]{1,0:T(8,128)(2,1)}, bf16[64,1024]{1,0:T(8,128)(2,1)S(1)}, u32[]{:S(2)}, u32[]{:S(2)}) %collective-permute-start.10) | collective-permute-done | bytes 131104 | tf_op jit(solution)/shard_map/ppermute | solution.py:93
  16.9 0.0 collective-permute-done.11
  16.9 1.6 %collective-permute-start.12 = (bf16[192,1024]{1,0:T(8,128)(2,1)S(1)}, bf16[192,1024]{1,0:T(8,128)(2,1)S(1)}, u32[]{:S(2)}, u32[]{:S(2)}) collective-permute-start(bf16[192,1024]{1,0:T(8,128)(2,1)S(1)} %constant_dynamic-update-slice_fusion.e0), channel_id=1, source_target_pairs={{0,1},{1,0},{2,3},{3,2},{4,6},{5,7},{6,4},{7,5},{8,9},{9,8},{10,11... | collective-permute-start | bytes 1179656 | tf_op jit(solution)/shard_map/ppermute | solution.py:93
  18.4 0.5 collective-permute-start.2
  19.0 0.9 %copy-done = bf16[1,64,1024]{2,1,0:T(8,128)(2,1)S(1)} copy-done((bf16[1,64,1024]{2,1,0:T(8,128)(2,1)S(1)}, bf16[1,64,1024]{2,1,0:T(8,128)(2,1)}, u32[]{:S(2)}) %copy-start) | copy-done | bytes 131096
  19.9 1.6 %collective-permute-start.13 = (bf16[192,1024]{1,0:T(8,128)(2,1)S(1)}, bf16[192,1024]{1,0:T(8,128)(2,1)S(1)}, u32[]{:S(2)}, u32[]{:S(2)}) collective-permute-start(bf16[192,1024]{1,0:T(8,128)(2,1)S(1)} %constant_dynamic-update-slice_fusion.e0), channel_id=1, source_target_pairs={{0,2},{1,3},{2,0},{3,1},{4,5},{5,4},{6,7},{7,6},{8,10},{9,11},{10,... | collective-permute-start | bytes 1179656 | tf_op jit(solution)/shard_map/ppermute | solution.py:93
  21.5 0.0 collective-permute-done.4.q_near
  21.5 0.6 collective-permute-start.5
  22.1 9.6 %collective-permute-done.2 = bf16[64,1024]{1,0:T(8,128)(2,1)S(1)} collective-permute-done((bf16[64,1024]{1,0:T(8,128)(2,1)}, bf16[64,1024]{1,0:T(8,128)(2,1)S(1)}, u32[]{:S(2)}, u32[]{:S(2)}) %collective-permute-start.2) | collective-permute-done | bytes 131104 | tf_op jit(solution)/shard_map/ppermute | solution.py:93
  31.8 1.6 %collective-permute-start.3 = (bf16[128,1024]{1,0:T(8,128)(2,1)S(1)}, bf16[128,1024]{1,0:T(8,128)(2,1)S(1)}, u32[]{:S(2)}, u32[]{:S(2)}) collective-permute-start(bf16[128,1024]{1,0:T(8,128)(2,1)S(1)} %constant_dynamic-update-slice_fusion.3.near.cnear), channel_id=1, source_target_pairs={{0,2},{1,3},{2,0},{3,1},{4,5},{5,4},{6,7},{7,6},{8,10},{9,11},{10,... | collective-permute-start | bytes 786440 | tf_op jit(solution)/shard_map/ppermute | solution.py:93
  33.3 0.0 collective-permute-done.12.e1
  33.4 0.5 collective-permute-start.14
  33.9 1.5 %collective-permute-start = (bf16[192,1024]{1,0:T(8,128)(2,1)S(1)}, bf16[192,1024]{1,0:T(8,128)(2,1)S(1)}, u32[]{:S(2)}, u32[]{:S(2)}) collective-permute-start(bf16[192,1024]{1,0:T(8,128)(2,1)S(1)} %get-tuple-element.23), channel_id=1, source_target_pairs={{0,1},{1,0},{2,3},{3,2},{4,6},{5,7},{6,4},{7,5},{8,9},{9,8},{10,11... | collective-permute-start | bytes 1179656 | tf_op jit(solution)/shard_map/ppermute | solution.py:93
  35.3 0.0 collective-permute-done.5.q_far
  35.4 0.8 %shard_map.90 = (bf16[256,256]{1,0:T(8,128)(2,1)S(1)}, bf16[256,256]{1,0:T(8,128)(2,1)S(1)}, bf16[256,256]{1,0:T(8,128)(2,1)S(1)}, bf16[256,256]{1,0:T(8,128)(2,1)S(1)}) custom-call(s32[1,1024]{1,0:T(1,128)S(1)} %copy-done.1, bf16[256,1024]{1,0:T(8,128)(2,1)S(1)} %get-tuple-element.22.t_ref, bf16[128,1024]{1,0:T(8,128)(2,1)S(1)} %collective-permute-done.4.q_near, ...), custom_call_target="tpu_custom_call" | custom-call | flops 536870912 | bytes 1048576 | tf_op jit(solution)/shard_map/pallas_call | solution.py:303
  36.1 1.8 %collective-permute-start.6 = (bf16[256,256]{1,0:T(8,128)(2,1)S(1)}, bf16[256,256]{1,0:T(8,128)(2,1)S(1)}, u32[]{:S(2)}, u32[]{:S(2)}) collective-permute-start(bf16[256,256]{1,0:T(8,128)(2,1)S(1)} %get-tuple-element.32), channel_id=1, source_target_pairs={{0,8},{1,9},{2,10},{3,11},{4,12},{5,13},{6,14},{7,15},{8,0},{9,1},... | collective-permute-start | bytes 393224 | tf_op jit(solution)/shard_map/ppermute | solution.py:93
  37.9 0.3 collective-permute-done.3.far.cfar
  38.2 2.9 %collective-permute-start.7 = (bf16[256,256]{1,0:T(8,128)(2,1)S(1)}, bf16[256,256]{1,0:T(8,128)(2,1)S(1)}, u32[]{:S(2)}, u32[]{:S(2)}) collective-permute-start(bf16[256,256]{1,0:T(8,128)(2,1)S(1)} %get-tuple-element.33), channel_id=1, source_target_pairs={{0,16},{1,17},{2,18},{3,19},{4,20},{5,21},{6,22},{7,23},{8,24},{9,... | collective-permute-start | bytes 393224 | tf_op jit(solution)/shard_map/ppermute | solution.py:93
  41.1 0.0 collective-permute-done.13.e2
  41.1 1.2 %collective-permute-start.8 = (bf16[256,256]{1,0:T(8,128)(2,1)S(1)}, bf16[256,256]{1,0:T(8,128)(2,1)S(1)}, u32[]{:S(2)}, u32[]{:S(2)}) collective-permute-start(bf16[256,256]{1,0:T(8,128)(2,1)S(1)} %get-tuple-element.34), channel_id=1, source_target_pairs={{0,24},{1,25},{2,26},{3,27},{4,28},{5,29},{6,30},{7,31},{8,16},{9,... | collective-permute-start | bytes 393224 | tf_op jit(solution)/shard_map/ppermute | solution.py:93
  42.3 0.2 collective-permute-done.6.m1
  42.5 7.2 %collective-permute-done.7.m2 = bf16[256,256]{1,0:T(8,128)(2,1)S(1)} collective-permute-done((bf16[256,256]{1,0:T(8,128)(2,1)S(1)}, bf16[256,256]{1,0:T(8,128)(2,1)S(1)}, u32[]{:S(2)}, u32[]{:S(2)}) %collective-permute-start.7) | collective-permute-done | bytes 131104 | tf_op jit(solution)/shard_map/ppermute | solution.py:93
  49.8 0.0 collective-permute-done.8.m3
  49.8 0.0 collective-permute-done.14.e3
  49.8 0.8 %shard_map.91 = (f32[128,1024]{1,0:T(8,128)S(1)}, f32[8,1024]{1,0:T(8,128)S(1)}, f32[136,1024]{1,0:T(8,128)S(1)}) custom-call(bf16[256,256]{1,0:T(8,128)(2,1)S(1)} %get-tuple-element.31.m0, bf16[256,256]{1,0:T(8,128)(2,1)S(1)} %collective-permute-done.6.m1, bf16[256,256]{1,0:T(8,128)(2,1)S(1)} %collective-permute-done.7.m2, ...), custom_call_target="tpu_custom_call" | custom-call | flops 536870912 | bytes 2097152 | tf_op jit(solution)/shard_map/pallas_call | solution.py:303
  50.6 0.1 collective-permute-start.15
  50.7 0.0 collective-permute-done.p_near
  50.7 1.6 %collective-permute-start.1 = (bf16[192,1024]{1,0:T(8,128)(2,1)S(1)}, bf16[192,1024]{1,0:T(8,128)(2,1)S(1)}, u32[]{:S(2)}, u32[]{:S(2)}) collective-permute-start(bf16[192,1024]{1,0:T(8,128)(2,1)S(1)} %slice_dynamic-update-slice_fusion), channel_id=1, source_target_pairs={{0,2},{1,3},{2,0},{3,1},{4,5},{5,4},{6,7},{7,6},{8,10},{9,11},{10,... | collective-permute-start | bytes 1179656 | tf_op jit(solution)/shard_map/ppermute | solution.py:93
  52.3 2.2 %shard_map.85 = (bf16[1024,1024]{1,0:T(8,128)(2,1)S(1)}, bf16[1024,1024]{1,0:T(8,128)(2,1)S(1)}) custom-call(bf16[4096,1024]{1,0:T(8,128)(2,1)} %w_hbm.3), custom_call_target="tpu_custom_call" | custom-call | flops 1024 | bytes 4194304 | tf_op jit(solution)/shard_map/pallas_call | solution.py:303
  54.6 0.0 copy-start.2
  54.6 2.2 %shard_map.86 = (bf16[1024,1024]{1,0:T(8,128)(2,1)S(1)}, bf16[1024,1024]{1,0:T(8,128)(2,1)S(1)}) custom-call(bf16[4096,1024]{1,0:T(8,128)(2,1)} %w_hbm.3), custom_call_target="tpu_custom_call" | custom-call | flops 1024 | bytes 4194304 | tf_op jit(solution)/shard_map/pallas_call | solution.py:303
  56.8 0.0 copy-done.2
  56.8 0.0 copy-start.3
  56.9 3.7 %shard_map.89 = bf16[256,1024]{1,0:T(8,128)(2,1)} custom-call(s32[1,1024]{1,0:T(1,128)S(1)} %copy-done.2, bf16[128,1024]{1,0:T(8,128)(2,1)S(1)} %constant_dynamic-update-slice_fusion.3.near.cnear, bf16[128,1024]{1,0:T(8,128)(2,1)S(1)} %collective-permute-done.3.far.cfar, bf16[1024,1024]{1,0:T(8,128)(2,1)S(1)} %get-tuple-element.25.w0, ...), custom_call_target="tpu_custom_call" | custom-call | flops 2684354560 | bytes 8388608 | tf_op jit(solution)/shard_map/pallas_call | solution.py:303
  60.6 0.0 collective-permute-done.1.p_far
  60.6 0.0 copy-done.3
  60.6 3.6 %shard_map.87 = bf16[64,1024]{1,0:T(8,128)(2,1)} custom-call(s32[1,1024]{1,0:T(1,128)S(1)} %copy-done.2, bf16[1024]{0:T(1024)(128)(2,1)S(1)} %copy-done.3, bf16[256,1024]{1,0:T(8,128)(2,1)S(1)} %get-tuple-element.22.t_ref, bf16[192,1024]{1,0:T(8,128)(2,1)S(1)} %collective-permute-done.p_near, bf16[192,1024]{1,0:T(8,128)(2,1)S(1)} %collective-permute-done.1.p_far, ...), custom_call_target="tpu_custom_call" | custom-call | flops 1073741824 | bytes 8388608 | tf_op jit(solution)/shard_map/pallas_call | solution.py:303
  64.2 0.0 collective-permute-done.15.taken
  64.2 0.9 %shard_map.92 = (f32[128,1024]{1,0:T(8,128)}, f32[1,1024]{1,0:T(1,128)}) custom-call(f32[128,1024]{1,0:T(8,128)S(1)} %get-tuple-element.35.keep, f32[8,1024]{1,0:T(8,128)S(1)} %get-tuple-element.36.keep_bias, f32[136,1024]{1,0:T(8,128)S(1)} %collective-permute-done.15.taken), custom_call_target="tpu_custom_call" | custom-call | flops 131072 | bytes 1572864 | tf_op jit(solution)/shard_map/pallas_call | solution.py:303
  (9 shorter events, 0.1 us)
Async XLA Ops:
  0.6 10.1 %collective-permute-start.9 = (bf16[64,1024]{1,0:T(8,128)(2,1)}, bf16[64,1024]{1,0:T(8,128)(2,1)S(1)}, u32[]{:S(2)}, u32[]{:S(2)}) collective-permute-start(bf16[64,1024]{1,0:T(8,128)(2,1)} %bitcast.5), channel_id=1, source_target_pairs={{0,8},{1,9},{2,10},{3,11},{4,12},{5,13},{6,14},{7,15},{8,0},{9,1},... | collective-permute-start | bytes 393224 | tf_op jit(solution)/shard_map/ppermute | solution.py:93
  3.7 13.1 %collective-permute-start.10 = (bf16[64,1024]{1,0:T(8,128)(2,1)}, bf16[64,1024]{1,0:T(8,128)(2,1)S(1)}, u32[]{:S(2)}, u32[]{:S(2)}) collective-permute-start(bf16[64,1024]{1,0:T(8,128)(2,1)} %bitcast.6), channel_id=1, source_target_pairs={{0,16},{1,17},{2,18},{3,19},{4,20},{5,21},{6,22},{7,23},{8,24},{9,... | collective-permute-start | bytes 393224 | tf_op jit(solution)/shard_map/ppermute | solution.py:93
  6.3 10.5 %collective-permute-start.11 = (bf16[64,1024]{1,0:T(8,128)(2,1)}, bf16[64,1024]{1,0:T(8,128)(2,1)S(1)}, u32[]{:S(2)}, u32[]{:S(2)}) collective-permute-start(bf16[64,1024]{1,0:T(8,128)(2,1)} %bitcast.7), channel_id=1, source_target_pairs={{0,24},{1,25},{2,26},{3,27},{4,28},{5,29},{6,30},{7,31},{8,16},{9,... | collective-permute-start | bytes 393224 | tf_op jit(solution)/shard_map/ppermute | solution.py:93
  6.3 0.7 %copy-start.1 = (s32[1,1024]{1,0:T(1,128)S(1)}, s32[1,1024]{1,0:T(1,128)}, u32[]{:S(2)}) copy-start(s32[1,1024]{1,0:T(1,128)} %order_ref.7) | copy-start | bytes 12292
  7.0 1.0 %copy-start.4 = (bf16[1,256,1024]{2,1,0:T(8,128)(2,1)S(1)}, bf16[1,256,1024]{2,1,0:T(8,128)(2,1)}, u32[]{:S(2)}) copy-start(bf16[1,256,1024]{2,1,0:T(8,128)(2,1)} %param.5) | copy-start | bytes 1572868
  8.9 12.6 %collective-permute-start.4 = (bf16[128,1024]{1,0:T(8,128)(2,1)S(1)}, bf16[128,1024]{1,0:T(8,128)(2,1)S(1)}, u32[]{:S(2)}, u32[]{:S(2)}) collective-permute-start(bf16[128,1024]{1,0:T(8,128)(2,1)S(1)} %get-tuple-element.29), channel_id=1, source_target_pairs={{0,1},{1,0},{2,3},{3,2},{4,6},{5,7},{6,4},{7,5},{8,9},{9,8},{10,11... | collective-permute-start | bytes 786440 | tf_op jit(solution)/shard_map/ppermute | solution.py:93
  16.9 16.5 %collective-permute-start.12 = (bf16[192,1024]{1,0:T(8,128)(2,1)S(1)}, bf16[192,1024]{1,0:T(8,128)(2,1)S(1)}, u32[]{:S(2)}, u32[]{:S(2)}) collective-permute-start(bf16[192,1024]{1,0:T(8,128)(2,1)S(1)} %constant_dynamic-update-slice_fusion.e0), channel_id=1, source_target_pairs={{0,1},{1,0},{2,3},{3,2},{4,6},{5,7},{6,4},{7,5},{8,9},{9,8},{10,11... | collective-permute-start | bytes 1179656 | tf_op jit(solution)/shard_map/ppermute | solution.py:93
  18.4 13.3 %collective-permute-start.2 = (bf16[64,1024]{1,0:T(8,128)(2,1)}, bf16[64,1024]{1,0:T(8,128)(2,1)S(1)}, u32[]{:S(2)}, u32[]{:S(2)}) collective-permute-start(bf16[64,1024]{1,0:T(8,128)(2,1)} %bitcast.8), channel_id=1, source_target_pairs={{0,1},{1,0},{2,3},{3,2},{4,6},{5,7},{6,4},{7,5},{8,9},{9,8},{10,11... | collective-permute-start | bytes 393224 | tf_op jit(solution)/shard_map/ppermute | solution.py:93
  19.0 0.9 %copy-start = (bf16[1,64,1024]{2,1,0:T(8,128)(2,1)S(1)}, bf16[1,64,1024]{2,1,0:T(8,128)(2,1)}, u32[]{:S(2)}) copy-start(bf16[1,64,1024]{2,1,0:T(8,128)(2,1)} %param.9) | copy-start | bytes 393220
  19.9 21.2 %collective-permute-start.13 = (bf16[192,1024]{1,0:T(8,128)(2,1)S(1)}, bf16[192,1024]{1,0:T(8,128)(2,1)S(1)}, u32[]{:S(2)}, u32[]{:S(2)}) collective-permute-start(bf16[192,1024]{1,0:T(8,128)(2,1)S(1)} %constant_dynamic-update-slice_fusion.e0), channel_id=1, source_target_pairs={{0,2},{1,3},{2,0},{3,1},{4,5},{5,4},{6,7},{7,6},{8,10},{9,11},{10,... | collective-permute-start | bytes 1179656 | tf_op jit(solution)/shard_map/ppermute | solution.py:93
  21.5 13.8 %collective-permute-start.5 = (bf16[128,1024]{1,0:T(8,128)(2,1)S(1)}, bf16[128,1024]{1,0:T(8,128)(2,1)S(1)}, u32[]{:S(2)}, u32[]{:S(2)}) collective-permute-start(bf16[128,1024]{1,0:T(8,128)(2,1)S(1)} %slice_dynamic-update-slice_fusion.1), channel_id=1, source_target_pairs={{0,2},{1,3},{2,0},{3,1},{4,5},{5,4},{6,7},{7,6},{8,10},{9,11},{10,... | collective-permute-start | bytes 786440 | tf_op jit(solution)/shard_map/ppermute | solution.py:93
  31.8 6.4 %collective-permute-start.3 = (bf16[128,1024]{1,0:T(8,128)(2,1)S(1)}, bf16[128,1024]{1,0:T(8,128)(2,1)S(1)}, u32[]{:S(2)}, u32[]{:S(2)}) collective-permute-start(bf16[128,1024]{1,0:T(8,128)(2,1)S(1)} %constant_dynamic-update-slice_fusion.3.near.cnear), channel_id=1, source_target_pairs={{0,2},{1,3},{2,0},{3,1},{4,5},{5,4},{6,7},{7,6},{8,10},{9,11},{10,... | collective-permute-start | bytes 786440 | tf_op jit(solution)/shard_map/ppermute | solution.py:93
  33.4 16.4 %collective-permute-start.14 = (bf16[192,1024]{1,0:T(8,128)(2,1)S(1)}, bf16[192,1024]{1,0:T(8,128)(2,1)S(1)}, u32[]{:S(2)}, u32[]{:S(2)}) collective-permute-start(bf16[192,1024]{1,0:T(8,128)(2,1)S(1)} %collective-permute-done.12.e1), channel_id=1, source_target_pairs={{0,2},{1,3},{2,0},{3,1},{4,5},{5,4},{6,7},{7,6},{8,10},{9,11},{10,... | collective-permute-start | bytes 1179656 | tf_op jit(solution)/shard_map/ppermute | solution.py:93
  33.9 16.8 %collective-permute-start = (bf16[192,1024]{1,0:T(8,128)(2,1)S(1)}, bf16[192,1024]{1,0:T(8,128)(2,1)S(1)}, u32[]{:S(2)}, u32[]{:S(2)}) collective-permute-start(bf16[192,1024]{1,0:T(8,128)(2,1)S(1)} %get-tuple-element.23), channel_id=1, source_target_pairs={{0,1},{1,0},{2,3},{3,2},{4,6},{5,7},{6,4},{7,5},{8,9},{9,8},{10,11... | collective-permute-start | bytes 1179656 | tf_op jit(solution)/shard_map/ppermute | solution.py:93
  36.1 6.4 %collective-permute-start.6 = (bf16[256,256]{1,0:T(8,128)(2,1)S(1)}, bf16[256,256]{1,0:T(8,128)(2,1)S(1)}, u32[]{:S(2)}, u32[]{:S(2)}) collective-permute-start(bf16[256,256]{1,0:T(8,128)(2,1)S(1)} %get-tuple-element.32), channel_id=1, source_target_pairs={{0,8},{1,9},{2,10},{3,11},{4,12},{5,13},{6,14},{7,15},{8,0},{9,1},... | collective-permute-start | bytes 393224 | tf_op jit(solution)/shard_map/ppermute | solution.py:93
  38.2 11.6 %collective-permute-start.7 = (bf16[256,256]{1,0:T(8,128)(2,1)S(1)}, bf16[256,256]{1,0:T(8,128)(2,1)S(1)}, u32[]{:S(2)}, u32[]{:S(2)}) collective-permute-start(bf16[256,256]{1,0:T(8,128)(2,1)S(1)} %get-tuple-element.33), channel_id=1, source_target_pairs={{0,16},{1,17},{2,18},{3,19},{4,20},{5,21},{6,22},{7,23},{8,24},{9,... | collective-permute-start | bytes 393224 | tf_op jit(solution)/shard_map/ppermute | solution.py:93
  41.1 8.7 %collective-permute-start.8 = (bf16[256,256]{1,0:T(8,128)(2,1)S(1)}, bf16[256,256]{1,0:T(8,128)(2,1)S(1)}, u32[]{:S(2)}, u32[]{:S(2)}) collective-permute-start(bf16[256,256]{1,0:T(8,128)(2,1)S(1)} %get-tuple-element.34), channel_id=1, source_target_pairs={{0,24},{1,25},{2,26},{3,27},{4,28},{5,29},{6,30},{7,31},{8,16},{9,... | collective-permute-start | bytes 393224 | tf_op jit(solution)/shard_map/ppermute | solution.py:93
  50.6 13.6 %collective-permute-start.15 = (f32[136,1024]{1,0:T(8,128)S(1)}, f32[136,1024]{1,0:T(8,128)S(1)}, u32[]{:S(2)}, u32[]{:S(2)}) collective-permute-start(f32[136,1024]{1,0:T(8,128)S(1)} %get-tuple-element.37), channel_id=1, source_target_pairs={{0,4},{1,5},{2,6},{3,7},{4,0},{5,1},{6,2},{7,3},{8,12},{9,13},{10,... | collective-permute-start | bytes 1671176 | tf_op jit(solution)/shard_map/ppermute | solution.py:93
  50.7 9.8 %collective-permute-start.1 = (bf16[192,1024]{1,0:T(8,128)(2,1)S(1)}, bf16[192,1024]{1,0:T(8,128)(2,1)S(1)}, u32[]{:S(2)}, u32[]{:S(2)}) collective-permute-start(bf16[192,1024]{1,0:T(8,128)(2,1)S(1)} %slice_dynamic-update-slice_fusion), channel_id=1, source_target_pairs={{0,2},{1,3},{2,0},{3,1},{4,5},{5,4},{6,7},{7,6},{8,10},{9,11},{10,... | collective-permute-start | bytes 1179656 | tf_op jit(solution)/shard_map/ppermute | solution.py:93
  54.6 2.3 %copy-start.2 = (s32[1,1024]{1,0:T(1,128)S(1)}, s32[1,1024]{1,0:T(1,128)}, u32[]{:S(2)}) copy-start(s32[1,1024]{1,0:T(1,128)} %order_ref.7) | copy-start | bytes 12292
  56.8 3.7 %copy-start.3 = (bf16[1024]{0:T(1024)(128)(2,1)S(1)}, bf16[1024]{0:T(1024)(128)(2,1)}, u32[]{:S(2)}) copy-start(bf16[1024]{0:T(1024)(128)(2,1)} %bias_ref.1) | copy-start | bytes 6148

commit v3 on v2

--- a/solution.py
+++ b/solution.py
@@ -138,10 +138,9 @@
     return [pl.multiple_of(s * group + c * SPANS * group, LANES) for c in range(2)]
 
 
-def pack_kernel(order_ref, t_in, t_ref, q_first, q_second, p_first, p_second):
+def channels_kernel(t_in, t_ref, q_first, q_second):
     tok_dev = t_in.shape[0]
     mrows = tok_dev // MERGE
-    slots = p_second.shape[0] // 2
     group = LANES
     s = lax.axis_index("span")
     _, h, g, d = band_offsets()
@@ -153,10 +152,17 @@
                 q[first:first + mrows, column:column + group] = t_in[
                     j * mrows:(j + 1) * mrows, pl.ds(start, group)
                 ]
+
+
+def pack_kernel(order_ref, t_ref, p_first, p_second):
+    tok_dev = t_ref.shape[0]
+    slots = p_second.shape[0] // 2
+    s = lax.axis_index("span")
+    _, h, g, d = band_offsets()
     order = order_row(order_ref, s, tok_dev)
     for o, p, first in ((h, p_first, 0), (d, p_first, slots), (g, p_second, 0)):
         hot = slot_hot(order, s ^ o, tok_dev, slots)
-        rows = jnp.dot(hot, t_in[...], preferred_element_type=jnp.float32)
+        rows = jnp.dot(hot, t_ref[...], preferred_element_type=jnp.float32)
         p[first:first + slots, :] = rows.astype(p.dtype)
 
 
@@ -199,26 +205,40 @@
         out[...] = jnp.dot(hot, slab, preferred_element_type=jnp.float32).astype(out.dtype)
 
 
-def forward_kernel(order_ref, bias_ref, t_ref, p_near, p_far, w0, w1, w2, w3, out):
+def place_hot(order_ref, raster, s, o, tok_dev, slots):
+    f32 = jnp.float32
+    order = order_row(order_ref, s ^ o, tok_dev)
+    held = slot_hot(order, s, tok_dev, slots)
+    place = jnp.where(order // tok_dev == s, order - s * tok_dev + 1, 0)
+    place = jnp.broadcast_to(place, (16, tok_dev)).astype(f32).astype(jnp.bfloat16)
+    held = lax.dot_general(place, held, (((1,), (1,)), ((), ())), preferred_element_type=f32)
+    return bf16_hot(raster - s * tok_dev + 1 == held[:1].astype(jnp.int32))
+
+
+def gather_kernel(order_ref, t_ref, p_near, mine_ref, hot_g, hot_d):
     tok_dev = t_ref.shape[0]
     mrows = tok_dev // MERGE
-    slots = p_far.shape[0] // 2
+    slots = p_near.shape[0] // 2
     s = lax.axis_index("span")
     _, h, g, d = band_offsets()
     f32 = jnp.float32
     local = lax.broadcasted_iota(jnp.int32, (tok_dev, 1), 0)
     raster = raster_of(local // mrows, s, local % mrows, tok_dev)
-    mine_order = order_row(order_ref, s, tok_dev)
-    mine = jnp.dot(bf16_hot(raster == mine_order), t_ref[...], preferred_element_type=f32)
-    key = raster - s * tok_dev + 1
-    for o, p, first in ((h, p_near, 0), (g, p_far, 0), (d, p_far, slots)):
-        order = order_row(order_ref, s ^ o, tok_dev)
-        held = slot_hot(order, s, tok_dev, slots)
-        place = jnp.where(order // tok_dev == s, order - s * tok_dev + 1, 0)
-        place = jnp.broadcast_to(place, (16, tok_dev)).astype(f32).astype(jnp.bfloat16)
-        held = lax.dot_general(place, held, (((1,), (1,)), ((), ())), preferred_element_type=f32)
-        hot = bf16_hot(key == held[:1].astype(jnp.int32))
-        mine += jnp.dot(hot, p[first:first + slots, :], preferred_element_type=f32)
+    hot = bf16_hot(raster == order_row(order_ref, s, tok_dev))
+    near = place_hot(order_ref, raster, s, h, tok_dev, slots)
+    mine = jnp.dot(hot, t_ref[...], preferred_element_type=f32)
+    mine_ref[...] = mine + jnp.dot(near, p_near[:slots, :], preferred_element_type=f32)
+    hot_g[...] = place_hot(order_ref, raster, s, g, tok_dev, slots)
+    hot_d[...] = place_hot(order_ref, raster, s, d, tok_dev, slots)
+
+
+def forward_kernel(bias_ref, mine_ref, hot_g, hot_d, p_far, w0, w1, w2, w3, out):
+    mrows = mine_ref.shape[0] // MERGE
+    slots = p_far.shape[0] // 2
+    f32 = jnp.float32
+    mine = mine_ref[...]
+    mine += jnp.dot(hot_g[...], p_far[:slots, :], preferred_element_type=f32)
+    mine += jnp.dot(hot_d[...], p_far[slots:, :], preferred_element_type=f32)
     mine = mine.astype(jnp.bfloat16)
     acc = bias_ref[...].astype(f32).reshape(1, -1)
     for k, w in enumerate((w0, w1, w2, w3)):
@@ -253,38 +273,74 @@
     ).astype(tgrad.dtype)
 
 
-def weight_kernel(m0, m1, m2, m3, cnear, cfar, e0, e1, e2, e3, keep, keep_bias, give):
+def split_rows(total):
+    group = total.shape[0] // 2
+    mine = lax.axis_index("view") % 2 == 0
+    low, high = total[:group], total[group:]
+    return jnp.where(mine, low, high), jnp.where(mine, high, low)
+
+
+def early_kernel(m0, m1, m2, m3, cnear, cfar, e0, e1, e2, keep, give, pair, third):
     mrows = cnear.shape[0] // 2
+    f32 = jnp.float32
+    ms = (m0, m1, m2, m3)
+    lhs = []
+    rhs = []
+    sums = []
+    for j, (c, e) in enumerate(((cnear, e0), (cnear, e1), (cfar, e2), (cfar, None))):
+        rows = c[(j % 2) * mrows:(j % 2 + 1) * mrows, :]
+        count = 1 if e is None else MERGE
+        lhs += [m[j * mrows:(j + 1) * mrows, :] for m in ms[:count]]
+        rhs.append(rows)
+        if e is not None:
+            rhs.append(e[...])
+            b = [e[i * mrows:(i + 1) * mrows, :].astype(f32) for i in range(MERGE - 1)]
+            sums.append((rows.astype(f32) + b[0]) + (b[1] + b[2]))
+    total = lax.dot_general(
+        jnp.concatenate(lhs, axis=0),
+        jnp.concatenate(rhs, axis=0),
+        (((0,), (0,)), ((), ())),
+        preferred_element_type=f32,
+    )
+    keep[...], give[...] = split_rows(total)
+    pair[...] = sums[0] + sums[1]
+    third[...] = sums[2]
+
+
+def last_rows(ms, theirs, mrows):
     core = lax.axis_index("view") % 2
-    f32 = jnp.float32
-
-    def stacked(j):
-        return jnp.concatenate(
-            [m[j * mrows:(j + 1) * mrows, :] for m in (m0, m1, m2, m3)], axis=0
-        )
-
-    lhs = jnp.concatenate([stacked(j) for j in range(SPANS)], axis=0)
-    blocks = []
-    for c, pair in ((cnear, (e0, e1)), (cfar, (e2, e3))):
-        for j, e in enumerate(pair):
-            blocks += [c[j * mrows:(j + 1) * mrows, :], e[...]]
-    rhs = jnp.concatenate(blocks, axis=0)
-    group = lhs.shape[1] // 2
-    total = lax.dot_general(lhs, rhs, (((0,), (0,)), ((), ())), preferred_element_type=f32)
-    low, high = total[:group], total[group:]
-    mine = core == 0
-    keep[...] = jnp.where(mine, low, high)
-    give[:group, :] = jnp.where(mine, high, low)
-    pieces = rhs.astype(f32).reshape(SPANS, MERGE, mrows, rhs.shape[1])
-
-    def block_sum(b):
-        return (b[0] + b[1]) + (b[2] + b[3])
-
-    sums = [block_sum(pieces[j]) for j in range(SPANS)]
-    tree = (sums[0] + sums[1]) + (sums[2] + sums[3])
-    bias = jnp.broadcast_to(jnp.sum(tree, axis=0, keepdims=True), keep_bias.shape)
-    keep_bias[...] = bias
+    group = ms[0].shape[1] // 2
+    start = pl.multiple_of((1 - core if theirs else core) * group, LANES)
+    first = (SPANS - 1) * mrows
+    return jnp.concatenate([m[first:first + mrows, pl.ds(start, group)] for m in ms], axis=0)
+
+
+def give_kernel(m1, m2, m3, cfar, e3, give_in, pair, third, give, bias_out):
+    mrows = cfar.shape[0] // 2
+    group = give_in.shape[0]
+    f32 = jnp.float32
+    give[:group, :] = give_in[...] + lax.dot_general(
+        last_rows((m1, m2, m3), True, mrows),
+        e3[...],
+        (((0,), (0,)), ((), ())),
+        preferred_element_type=f32,
+    )
+    b = [e3[i * mrows:(i + 1) * mrows, :].astype(f32) for i in range(MERGE - 1)]
+    fourth = (cfar[mrows:, :].astype(f32) + b[0]) + (b[1] + b[2])
+    tree = pair[...] + (third[...] + fourth)
+    bias = jnp.broadcast_to(jnp.sum(tree, axis=0, keepdims=True), bias_out.shape)
+    bias_out[...] = bias
     give[group:, :] = bias
+
+
+def keep_kernel(m1, m2, m3, e3, keep_in, keep):
+    mrows = e3.shape[0] // (MERGE - 1)
+    keep[...] = keep_in[...] + lax.dot_general(
+        last_rows((m1, m2, m3), False, mrows),
+        e3[...],
+        (((0,), (0,)), ((), ())),
+        preferred_element_type=jnp.float32,
+    )
 
 
 def finish_kernel(scale, keep, keep_bias, taken, weight_grad, bias_grad):
@@ -337,16 +393,16 @@
     capacity = 3 * (tok_dev // spans) // 2
     c1 = hop(c0, span_offset=first)
     zs = [hop(c0, view_offset=2 * dz) for dz in range(1, MERGE)]
-    tv, q_first, q_second, p_first, p_second = call(
+    tv, q_first, q_second = call(
+        channels_kernel,
+        (t0,),
+        [shape(tok_dev, width)] + [shape(2 * mrows, width)] * 2,
+        cost_of(tok_dev * width, 8 * tok_dev * width),
+    )
+    p_first, p_second = call(
         pack_kernel,
-        (scan_order, t0),
-        [
-            shape(tok_dev, width),
-            shape(2 * mrows, width),
-            shape(2 * mrows, width),
-            shape(2 * capacity, width),
-            shape(2 * capacity, width),
-        ],
+        (scan_order, tv),
+        [shape(2 * capacity, width)] * 2,
         cost_of(2 * 3 * capacity * tok_dev * width, 4 * tok_dev * width),
     )
     q_near = hop(q_first, span_offset=first)
@@ -386,19 +442,38 @@
         [shape(tok_dev, width)],
         cost_of(10 * tok_dev * width * width, 8 * width * width),
     )
+    mine, hot_g, hot_d = call(
+        gather_kernel,
+        (scan_order, tv, p_near),
+        [shape(tok_dev, width, f32)] + [shape(tok_dev, capacity)] * 2,
+        cost_of(4 * tok_dev * tok_dev * width, 4 * tok_dev * width),
+    )
     (merged_out,) = call(
         forward_kernel,
-        (scan_order, bias, tv, p_near, p_far, *weights),
+        (bias, mine, hot_g, hot_d, p_far, *weights),
         [shape(mrows, width)],
         cost_of(4 * tok_dev * width * width, 8 * width * width),
     )
-    keep, keep_bias, give = call(
-        weight_kernel,
-        (*ms, cnear, cfar, extra, e1, e2, e3),
-        [shape(group, width, f32), shape(8, width, f32), shape(group + 8, width, f32)],
+    wide = shape(group, width, f32)
+    keep, give, pair, third = call(
+        early_kernel,
+        (*ms, cnear, cfar, extra, e1, e2),
+        [wide, wide] + [shape(mrows, width, f32)] * 2,
         cost_of(4 * spans * tok_dev * group * width, 8 * tok_dev * width),
     )
+    give, keep_bias = call(
+        give_kernel,
+        (*ms[1:], cfar, e3, give, pair, third),
+        [shape(group + 8, width, f32), shape(8, width, f32)],
+        cost_of(2 * tok_dev * group * width, 4 * tok_dev * width),
+    )
     taken = hop(give, view_offset=1)
+    (keep,) = call(
+        keep_kernel,
+        (*ms[1:], e3, keep),
+        [wide],
+        cost_of(2 * tok_dev * group * width, 4 * tok_dev * width),
+    )
     scale = 1.0 / math.sqrt(views * spans * mrows)
     weight_grad, bias_grad = call(
         functools.partial(finish_kernel, scale),

time: 65.3 us -> 65.6 us (level)
  waiting for transfers between devices: 23.6 us -> 24.6 us
  local copies, waits for them, and re-layouts: 2.74 us -> 2.05 us
    ppermute x16, waiting for transfers between devices: 23.6 us -> 24.6 us  [xor_permute(): return lax.ppermute(x, ('view', 'span'), pairs)]
    unnamed x12 -> x10, local copies, waits for them, and re-layouts: 2.7 us -> 2.01 us
    pallas_call x9 -> x13, Pallas kernels: 15.1 us -> 15.5 us  [call(): pl.pallas_call(kernel, out_shape=outs, in_specs=[far if i in hbm else vme...]
  transfers between devices with their start and end apart: 16 -> 16, of which waited for: 5 -> 4; matrix products, arithmetic and copies ran while one was open for 0% -> 0% of each run, Pallas kernels for 22% -> 22%
where the time goes in v3:
time: 65.6 us; the launch traced here: 65.4 us
  waiting for transfers between devices  24.6 us (38%)
  starting transfers between devices  22.4 us (34%)
  Pallas kernels  15.5 us (24%)
  local copies, waits for them, and re-layouts  2.05 us (3%)
  between operations  0.8 us (1%)
    ppermute x16, waiting for transfers between devices, xor_permute(): return lax.ppermute(x, ('view', 'span'), pairs)  24.6 us
    ppermute x16, starting transfers between devices, xor_permute(): return lax.ppermute(x, ('view', 'span'), pairs)  22.4 us
    pallas_call x13, Pallas kernels, call(): pl.pallas_call(kernel, out_shape=outs, in_specs=[far if i in hbm else vme...  15.5 us
    unnamed x10, local copies, waits for them, and re-layouts  2.01 us
  transfers between devices with their start and end apart: 16, of which 4 were waited for; matrix products, arithmetic and copies ran while one was open for 0% of the time, Pallas kernels for 22%

profile of v3, /device:TPU:0, one launch (start us, length us, event | category | flops | bytes accessed | tf_op | source)
XLA Modules:
  0.0 65.4 jit_solution(15340474649852544352)
XLA Ops:
  0.6 3.1 %collective-permute-start.9 = (bf16[64,1024]{1,0:T(8,128)(2,1)}, bf16[64,1024]{1,0:T(8,128)(2,1)S(1)}, u32[]{:S(2)}, u32[]{:S(2)}) collective-permute-start(bf16[64,1024]{1,0:T(8,128)(2,1)} %bitcast.6), channel_id=1, source_target_pairs={{0,8},{1,9},{2,10},{3,11},{4,12},{5,13},{6,14},{7,15},{8,0},{9,1},... | collective-permute-start | bytes 393224 | tf_op jit(solution)/shard_map/ppermute | solution.py:93
  3.7 2.6 %collective-permute-start.10 = (bf16[64,1024]{1,0:T(8,128)(2,1)}, bf16[64,1024]{1,0:T(8,128)(2,1)S(1)}, u32[]{:S(2)}, u32[]{:S(2)}) collective-permute-start(bf16[64,1024]{1,0:T(8,128)(2,1)} %bitcast.7), channel_id=1, source_target_pairs={{0,16},{1,17},{2,18},{3,19},{4,20},{5,21},{6,22},{7,23},{8,24},{9,... | collective-permute-start | bytes 393224 | tf_op jit(solution)/shard_map/ppermute | solution.py:93
  6.3 0.0 collective-permute-start.11
  6.3 1.0 %copy-done = bf16[1,256,1024]{2,1,0:T(8,128)(2,1)S(1)} copy-done((bf16[1,256,1024]{2,1,0:T(8,128)(2,1)S(1)}, bf16[1,256,1024]{2,1,0:T(8,128)(2,1)}, u32[]{:S(2)}) %copy-start) | copy-done | bytes 524312
  7.4 0.1 shard_map.84
  7.5 1.8 %collective-permute-start.4 = (bf16[128,1024]{1,0:T(8,128)(2,1)S(1)}, bf16[128,1024]{1,0:T(8,128)(2,1)S(1)}, u32[]{:S(2)}, u32[]{:S(2)}) collective-permute-start(bf16[128,1024]{1,0:T(8,128)(2,1)S(1)} %get-tuple-element.38), channel_id=1, source_target_pairs={{0,1},{1,0},{2,3},{3,2},{4,6},{5,7},{6,4},{7,5},{8,9},{9,8},{10,11... | collective-permute-start | bytes 786440 | tf_op jit(solution)/shard_map/ppermute | solution.py:93
  9.3 0.0 collective-permute-done.9
  9.3 7.5 %collective-permute-done.10 = bf16[64,1024]{1,0:T(8,128)(2,1)S(1)} collective-permute-done((bf16[64,1024]{1,0:T(8,128)(2,1)}, bf16[64,1024]{1,0:T(8,128)(2,1)S(1)}, u32[]{:S(2)}, u32[]{:S(2)}) %collective-permute-start.10) | collective-permute-done | bytes 131104 | tf_op jit(solution)/shard_map/ppermute | solution.py:93
  16.9 0.0 collective-permute-done.11
  16.9 1.6 %collective-permute-start.12 = (bf16[192,1024]{1,0:T(8,128)(2,1)S(1)}, bf16[192,1024]{1,0:T(8,128)(2,1)S(1)}, u32[]{:S(2)}, u32[]{:S(2)}) collective-permute-start(bf16[192,1024]{1,0:T(8,128)(2,1)S(1)} %constant_dynamic-update-slice_fusion.e0), channel_id=1, source_target_pairs={{0,1},{1,0},{2,3},{3,2},{4,6},{5,7},{6,4},{7,5},{8,9},{9,8},{10,11... | collective-permute-start | bytes 1179656 | tf_op jit(solution)/shard_map/ppermute | solution.py:93
  18.4 0.5 collective-permute-start.2
  19.0 0.9 %copy-done.1 = bf16[1,64,1024]{2,1,0:T(8,128)(2,1)S(1)} copy-done((bf16[1,64,1024]{2,1,0:T(8,128)(2,1)S(1)}, bf16[1,64,1024]{2,1,0:T(8,128)(2,1)}, u32[]{:S(2)}) %copy-start.1) | copy-done | bytes 131096
  19.9 1.6 %collective-permute-start.14 = (bf16[192,1024]{1,0:T(8,128)(2,1)S(1)}, bf16[192,1024]{1,0:T(8,128)(2,1)S(1)}, u32[]{:S(2)}, u32[]{:S(2)}) collective-permute-start(bf16[192,1024]{1,0:T(8,128)(2,1)S(1)} %constant_dynamic-update-slice_fusion.e0), channel_id=1, source_target_pairs={{0,2},{1,3},{2,0},{3,1},{4,5},{5,4},{6,7},{7,6},{8,10},{9,11},{10,... | collective-permute-start | bytes 1179656 | tf_op jit(solution)/shard_map/ppermute | solution.py:93
  21.5 0.0 collective-permute-done.4.q_near
  21.5 0.6 collective-permute-start.5
  22.1 9.6 %collective-permute-done.2 = bf16[64,1024]{1,0:T(8,128)(2,1)S(1)} collective-permute-done((bf16[64,1024]{1,0:T(8,128)(2,1)}, bf16[64,1024]{1,0:T(8,128)(2,1)S(1)}, u32[]{:S(2)}, u32[]{:S(2)}) %collective-permute-start.2) | collective-permute-done | bytes 131104 | tf_op jit(solution)/shard_map/ppermute | solution.py:93
  31.8 1.6 %collective-permute-start.3 = (bf16[128,1024]{1,0:T(8,128)(2,1)S(1)}, bf16[128,1024]{1,0:T(8,128)(2,1)S(1)}, u32[]{:S(2)}, u32[]{:S(2)}) collective-permute-start(bf16[128,1024]{1,0:T(8,128)(2,1)S(1)} %constant_dynamic-update-slice_fusion.3.near.cnear), channel_id=1, source_target_pairs={{0,2},{1,3},{2,0},{3,1},{4,5},{5,4},{6,7},{7,6},{8,10},{9,11},{10,... | collective-permute-start | bytes 786440 | tf_op jit(solution)/shard_map/ppermute | solution.py:93
  33.3 0.0 collective-permute-done.12.e1
  33.4 0.5 collective-permute-start.13
  33.9 0.8 %shard_map.85 = (bf16[192,1024]{1,0:T(8,128)(2,1)S(1)}, bf16[192,1024]{1,0:T(8,128)(2,1)S(1)}) custom-call(s32[1,1024]{1,0:T(1,128)S(1)} %copy-done.3, bf16[256,1024]{1,0:T(8,128)(2,1)S(1)} %get-tuple-element.28.t_ref), custom_call_target="tpu_custom_call" | custom-call | flops 150994944 | bytes 1048576 | tf_op jit(solution)/shard_map/pallas_call | solution.py:359
  34.6 1.6 %collective-permute-start = (bf16[192,1024]{1,0:T(8,128)(2,1)S(1)}, bf16[192,1024]{1,0:T(8,128)(2,1)S(1)}, u32[]{:S(2)}, u32[]{:S(2)}) collective-permute-start(bf16[192,1024]{1,0:T(8,128)(2,1)S(1)} %get-tuple-element.29), channel_id=1, source_target_pairs={{0,1},{1,0},{2,3},{3,2},{4,6},{5,7},{6,4},{7,5},{8,9},{9,8},{10,11... | collective-permute-start | bytes 1179656 | tf_op jit(solution)/shard_map/ppermute | solution.py:93
  36.2 0.0 collective-permute-done.5.q_far
  36.2 0.7 %shard_map.92 = (bf16[256,256]{1,0:T(8,128)(2,1)S(1)}, bf16[256,256]{1,0:T(8,128)(2,1)S(1)}, bf16[256,256]{1,0:T(8,128)(2,1)S(1)}, bf16[256,256]{1,0:T(8,128)(2,1)S(1)}) custom-call(s32[1,1024]{1,0:T(1,128)S(1)} %copy-done.3, bf16[256,1024]{1,0:T(8,128)(2,1)S(1)} %get-tuple-element.28.t_ref, bf16[128,1024]{1,0:T(8,128)(2,1)S(1)} %collective-permute-done.4.q_near, ...), custom_call_target="tpu_custom_call" | custom-call | flops 536870912 | bytes 1048576 | tf_op jit(solution)/shard_map/pallas_call | solution.py:359
  37.0 1.8 %collective-permute-start.6 = (bf16[256,256]{1,0:T(8,128)(2,1)S(1)}, bf16[256,256]{1,0:T(8,128)(2,1)S(1)}, u32[]{:S(2)}, u32[]{:S(2)}) collective-permute-start(bf16[256,256]{1,0:T(8,128)(2,1)S(1)} %get-tuple-element.40), channel_id=1, source_target_pairs={{0,8},{1,9},{2,10},{3,11},{4,12},{5,13},{6,14},{7,15},{8,0},{9,1},... | collective-permute-start | bytes 393224 | tf_op jit(solution)/shard_map/ppermute | solution.py:93
  38.7 0.0 collective-permute-done.3.far.cfar
  38.7 2.4 %collective-permute-start.7 = (bf16[256,256]{1,0:T(8,128)(2,1)S(1)}, bf16[256,256]{1,0:T(8,128)(2,1)S(1)}, u32[]{:S(2)}, u32[]{:S(2)}) collective-permute-start(bf16[256,256]{1,0:T(8,128)(2,1)S(1)} %get-tuple-element.41), channel_id=1, source_target_pairs={{0,16},{1,17},{2,18},{3,19},{4,20},{5,21},{6,22},{7,23},{8,24},{9,... | collective-permute-start | bytes 393224 | tf_op jit(solution)/shard_map/ppermute | solution.py:93
  41.1 0.0 collective-permute-done.14.e2
  41.1 1.2 %collective-permute-start.8 = (bf16[256,256]{1,0:T(8,128)(2,1)S(1)}, bf16[256,256]{1,0:T(8,128)(2,1)S(1)}, u32[]{:S(2)}, u32[]{:S(2)}) collective-permute-start(bf16[256,256]{1,0:T(8,128)(2,1)S(1)} %get-tuple-element.42), channel_id=1, source_target_pairs={{0,24},{1,25},{2,26},{3,27},{4,28},{5,29},{6,30},{7,31},{8,16},{9,... | collective-permute-start | bytes 393224 | tf_op jit(solution)/shard_map/ppermute | solution.py:93
  42.3 0.3 collective-permute-done.6.m1
  42.6 7.1 %collective-permute-done.7.m2 = bf16[256,256]{1,0:T(8,128)(2,1)S(1)} collective-permute-done((bf16[256,256]{1,0:T(8,128)(2,1)S(1)}, bf16[256,256]{1,0:T(8,128)(2,1)S(1)}, u32[]{:S(2)}, u32[]{:S(2)}) %collective-permute-start.7) | collective-permute-done | bytes 131104 | tf_op jit(solution)/shard_map/ppermute | solution.py:93
  49.7 0.0 collective-permute-done.8.m3
  49.8 0.7 %shard_map.93 = (f32[128,1024]{1,0:T(8,128)S(1)}, f32[128,1024]{1,0:T(8,128)S(1)}, f32[64,1024]{1,0:T(8,128)S(1)}, f32[64,1024]{1,0:T(8,128)S(1)}) custom-call(bf16[256,256]{1,0:T(8,128)(2,1)S(1)} %get-tuple-element.43.m0, bf16[256,256]{1,0:T(8,128)(2,1)S(1)} %collective-permute-done.6.m1, bf16[256,256]{1,0:T(8,128)(2,1)S(1)} %collective-permute-done.7.m2, ...), custom_call_target="tpu_custom_call" | custom-call | flops 536870912 | bytes 2097152 | tf_op jit(solution)/shard_map/pallas_call | solution.py:359
  50.5 0.0 collective-permute-done.13.e3
  50.5 0.3 shard_map.95
  50.9 0.1 collective-permute-start.15
  51.0 0.0 collective-permute-done.p_near
  51.0 1.6 %collective-permute-start.1 = (bf16[192,1024]{1,0:T(8,128)(2,1)S(1)}, bf16[192,1024]{1,0:T(8,128)(2,1)S(1)}, u32[]{:S(2)}, u32[]{:S(2)}) collective-permute-start(bf16[192,1024]{1,0:T(8,128)(2,1)S(1)} %slice_dynamic-update-slice_fusion), channel_id=1, source_target_pairs={{0,2},{1,3},{2,0},{3,1},{4,5},{5,4},{6,7},{7,6},{8,10},{9,11},{10,... | collective-permute-start | bytes 1179656 | tf_op jit(solution)/shard_map/ppermute | solution.py:93
  52.6 2.2 %shard_map.87 = (bf16[1024,1024]{1,0:T(8,128)(2,1)S(1)}, bf16[1024,1024]{1,0:T(8,128)(2,1)S(1)}) custom-call(bf16[4096,1024]{1,0:T(8,128)(2,1)} %w_hbm.3), custom_call_target="tpu_custom_call" | custom-call | flops 1024 | bytes 4194304 | tf_op jit(solution)/shard_map/pallas_call | solution.py:359
  54.8 2.2 %shard_map.88 = (bf16[1024,1024]{1,0:T(8,128)(2,1)S(1)}, bf16[1024,1024]{1,0:T(8,128)(2,1)S(1)}) custom-call(bf16[4096,1024]{1,0:T(8,128)(2,1)} %w_hbm.3), custom_call_target="tpu_custom_call" | custom-call | flops 1024 | bytes 4194304 | tf_op jit(solution)/shard_map/pallas_call | solution.py:359
  57.1 0.0 copy-start.2
  57.1 3.7 %shard_map.91 = bf16[256,1024]{1,0:T(8,128)(2,1)} custom-call(s32[1,1024]{1,0:T(1,128)S(1)} %copy-done.3, bf16[128,1024]{1,0:T(8,128)(2,1)S(1)} %constant_dynamic-update-slice_fusion.3.near.cnear, bf16[128,1024]{1,0:T(8,128)(2,1)S(1)} %collective-permute-done.3.far.cfar, bf16[1024,1024]{1,0:T(8,128)(2,1)S(1)} %get-tuple-element.34.w0, ...), custom_call_target="tpu_custom_call" | custom-call | flops 2684354560 | bytes 8388608 | tf_op jit(solution)/shard_map/pallas_call | solution.py:359
  60.8 0.9 %shard_map.86 = (f32[256,1024]{1,0:T(8,128)S(1)}, bf16[256,96]{1,0:T(8,128)(2,1)S(1)}, bf16[256,96]{1,0:T(8,128)(2,1)S(1)}) custom-call(s32[1,1024]{1,0:T(1,128)S(1)} %copy-done.3, bf16[256,1024]{1,0:T(8,128)(2,1)S(1)} %get-tuple-element.28.t_ref, bf16[192,1024]{1,0:T(8,128)(2,1)S(1)} %collective-permute-done.p_near), custom_call_target="tpu_custom_call" | custom-call | flops 268435456 | bytes 1048576 | tf_op jit(solution)/shard_map/pallas_call | solution.py:359
  61.7 0.0 collective-permute-done.1.p_far
  61.7 0.0 copy-done.2
  61.7 2.5 %shard_map.89 = bf16[64,1024]{1,0:T(8,128)(2,1)} custom-call(bf16[1024]{0:T(1024)(128)(2,1)S(1)} %copy-done.2, f32[256,1024]{1,0:T(8,128)S(1)} %get-tuple-element.30.mine_ref, bf16[256,96]{1,0:T(8,128)(2,1)S(1)} %get-tuple-element.31.hot_g, bf16[256,96]{1,0:T(8,128)(2,1)S(1)} %get-tuple-element.32.hot_d, bf16[192,1024]{1,0:T(8,128)(2,1)S(1)} %collective-permute-done.1.p_far, ...), custom_call_target="tpu_custom_call" | custom-call | flops 1073741824 | bytes 8388608 | tf_op jit(solution)/shard_map/pallas_call | solution.py:359
  64.3 0.3 shard_map.94.keep
  64.5 0.0 collective-permute-done.15.taken
  64.6 0.9 %shard_map.96 = (f32[128,1024]{1,0:T(8,128)}, f32[1,1024]{1,0:T(1,128)}) custom-call(f32[128,1024]{1,0:T(8,128)S(1)} %shard_map.94.keep, f32[8,1024]{1,0:T(8,128)S(1)} %get-tuple-element.48.keep_bias, f32[136,1024]{1,0:T(8,128)S(1)} %collective-permute-done.15.taken), custom_call_target="tpu_custom_call" | custom-call | flops 131072 | bytes 1572864 | tf_op jit(solution)/shard_map/pallas_call | solution.py:359
  (11 shorter events, 0.1 us)
Async XLA Ops:
  0.6 8.7 %collective-permute-start.9 = (bf16[64,1024]{1,0:T(8,128)(2,1)}, bf16[64,1024]{1,0:T(8,128)(2,1)S(1)}, u32[]{:S(2)}, u32[]{:S(2)}) collective-permute-start(bf16[64,1024]{1,0:T(8,128)(2,1)} %bitcast.6), channel_id=1, source_target_pairs={{0,8},{1,9},{2,10},{3,11},{4,12},{5,13},{6,14},{7,15},{8,0},{9,1},... | collective-permute-start | bytes 393224 | tf_op jit(solution)/shard_map/ppermute | solution.py:93
  3.7 13.1 %collective-permute-start.10 = (bf16[64,1024]{1,0:T(8,128)(2,1)}, bf16[64,1024]{1,0:T(8,128)(2,1)S(1)}, u32[]{:S(2)}, u32[]{:S(2)}) collective-permute-start(bf16[64,1024]{1,0:T(8,128)(2,1)} %bitcast.7), channel_id=1, source_target_pairs={{0,16},{1,17},{2,18},{3,19},{4,20},{5,21},{6,22},{7,23},{8,24},{9,... | collective-permute-start | bytes 393224 | tf_op jit(solution)/shard_map/ppermute | solution.py:93
  6.3 10.5 %collective-permute-start.11 = (bf16[64,1024]{1,0:T(8,128)(2,1)}, bf16[64,1024]{1,0:T(8,128)(2,1)S(1)}, u32[]{:S(2)}, u32[]{:S(2)}) collective-permute-start(bf16[64,1024]{1,0:T(8,128)(2,1)} %bitcast.8), channel_id=1, source_target_pairs={{0,24},{1,25},{2,26},{3,27},{4,28},{5,29},{6,30},{7,31},{8,16},{9,... | collective-permute-start | bytes 393224 | tf_op jit(solution)/shard_map/ppermute | solution.py:93
  6.3 1.0 %copy-start = (bf16[1,256,1024]{2,1,0:T(8,128)(2,1)S(1)}, bf16[1,256,1024]{2,1,0:T(8,128)(2,1)}, u32[]{:S(2)}) copy-start(bf16[1,256,1024]{2,1,0:T(8,128)(2,1)} %param.5) | copy-start | bytes 1572868
  7.4 26.5 %copy-start.3 = (s32[1,1024]{1,0:T(1,128)S(1)}, s32[1,1024]{1,0:T(1,128)}, u32[]{:S(2)}) copy-start(s32[1,1024]{1,0:T(1,128)} %order_ref.7) | copy-start | bytes 12292
  7.5 14.0 %collective-permute-start.4 = (bf16[128,1024]{1,0:T(8,128)(2,1)S(1)}, bf16[128,1024]{1,0:T(8,128)(2,1)S(1)}, u32[]{:S(2)}, u32[]{:S(2)}) collective-permute-start(bf16[128,1024]{1,0:T(8,128)(2,1)S(1)} %get-tuple-element.38), channel_id=1, source_target_pairs={{0,1},{1,0},{2,3},{3,2},{4,6},{5,7},{6,4},{7,5},{8,9},{9,8},{10,11... | collective-permute-start | bytes 786440 | tf_op jit(solution)/shard_map/ppermute | solution.py:93
  16.9 16.5 %collective-permute-start.12 = (bf16[192,1024]{1,0:T(8,128)(2,1)S(1)}, bf16[192,1024]{1,0:T(8,128)(2,1)S(1)}, u32[]{:S(2)}, u32[]{:S(2)}) collective-permute-start(bf16[192,1024]{1,0:T(8,128)(2,1)S(1)} %constant_dynamic-update-slice_fusion.e0), channel_id=1, source_target_pairs={{0,1},{1,0},{2,3},{3,2},{4,6},{5,7},{6,4},{7,5},{8,9},{9,8},{10,11... | collective-permute-start | bytes 1179656 | tf_op jit(solution)/shard_map/ppermute | solution.py:93
  18.4 13.3 %collective-permute-start.2 = (bf16[64,1024]{1,0:T(8,128)(2,1)}, bf16[64,1024]{1,0:T(8,128)(2,1)S(1)}, u32[]{:S(2)}, u32[]{:S(2)}) collective-permute-start(bf16[64,1024]{1,0:T(8,128)(2,1)} %bitcast.9), channel_id=1, source_target_pairs={{0,1},{1,0},{2,3},{3,2},{4,6},{5,7},{6,4},{7,5},{8,9},{9,8},{10,11... | collective-permute-start | bytes 393224 | tf_op jit(solution)/shard_map/ppermute | solution.py:93
  19.0 0.9 %copy-start.1 = (bf16[1,64,1024]{2,1,0:T(8,128)(2,1)S(1)}, bf16[1,64,1024]{2,1,0:T(8,128)(2,1)}, u32[]{:S(2)}) copy-start(bf16[1,64,1024]{2,1,0:T(8,128)(2,1)} %param.9) | copy-start | bytes 393220
  19.9 21.2 %collective-permute-start.14 = (bf16[192,1024]{1,0:T(8,128)(2,1)S(1)}, bf16[192,1024]{1,0:T(8,128)(2,1)S(1)}, u32[]{:S(2)}, u32[]{:S(2)}) collective-permute-start(bf16[192,1024]{1,0:T(8,128)(2,1)S(1)} %constant_dynamic-update-slice_fusion.e0), channel_id=1, source_target_pairs={{0,2},{1,3},{2,0},{3,1},{4,5},{5,4},{6,7},{7,6},{8,10},{9,11},{10,... | collective-permute-start | bytes 1179656 | tf_op jit(solution)/shard_map/ppermute | solution.py:93
  21.5 14.7 %collective-permute-start.5 = (bf16[128,1024]{1,0:T(8,128)(2,1)S(1)}, bf16[128,1024]{1,0:T(8,128)(2,1)S(1)}, u32[]{:S(2)}, u32[]{:S(2)}) collective-permute-start(bf16[128,1024]{1,0:T(8,128)(2,1)S(1)} %slice_dynamic-update-slice_fusion.1), channel_id=1, source_target_pairs={{0,2},{1,3},{2,0},{3,1},{4,5},{5,4},{6,7},{7,6},{8,10},{9,11},{10,... | collective-permute-start | bytes 786440 | tf_op jit(solution)/shard_map/ppermute | solution.py:93
  31.8 7.0 %collective-permute-start.3 = (bf16[128,1024]{1,0:T(8,128)(2,1)S(1)}, bf16[128,1024]{1,0:T(8,128)(2,1)S(1)}, u32[]{:S(2)}, u32[]{:S(2)}) collective-permute-start(bf16[128,1024]{1,0:T(8,128)(2,1)S(1)} %constant_dynamic-update-slice_fusion.3.near.cnear), channel_id=1, source_target_pairs={{0,2},{1,3},{2,0},{3,1},{4,5},{5,4},{6,7},{7,6},{8,10},{9,11},{10,... | collective-permute-start | bytes 786440 | tf_op jit(solution)/shard_map/ppermute | solution.py:93
  33.4 17.2 %collective-permute-start.13 = (bf16[192,1024]{1,0:T(8,128)(2,1)S(1)}, bf16[192,1024]{1,0:T(8,128)(2,1)S(1)}, u32[]{:S(2)}, u32[]{:S(2)}) collective-permute-start(bf16[192,1024]{1,0:T(8,128)(2,1)S(1)} %collective-permute-done.12.e1), channel_id=1, source_target_pairs={{0,2},{1,3},{2,0},{3,1},{4,5},{5,4},{6,7},{7,6},{8,10},{9,11},{10,... | collective-permute-start | bytes 1179656 | tf_op jit(solution)/shard_map/ppermute | solution.py:93
  34.6 16.3 %collective-permute-start = (bf16[192,1024]{1,0:T(8,128)(2,1)S(1)}, bf16[192,1024]{1,0:T(8,128)(2,1)S(1)}, u32[]{:S(2)}, u32[]{:S(2)}) collective-permute-start(bf16[192,1024]{1,0:T(8,128)(2,1)S(1)} %get-tuple-element.29), channel_id=1, source_target_pairs={{0,1},{1,0},{2,3},{3,2},{4,6},{5,7},{6,4},{7,5},{8,9},{9,8},{10,11... | collective-permute-start | bytes 1179656 | tf_op jit(solution)/shard_map/ppermute | solution.py:93
  37.0 5.7 %collective-permute-start.6 = (bf16[256,256]{1,0:T(8,128)(2,1)S(1)}, bf16[256,256]{1,0:T(8,128)(2,1)S(1)}, u32[]{:S(2)}, u32[]{:S(2)}) collective-permute-start(bf16[256,256]{1,0:T(8,128)(2,1)S(1)} %get-tuple-element.40), channel_id=1, source_target_pairs={{0,8},{1,9},{2,10},{3,11},{4,12},{5,13},{6,14},{7,15},{8,0},{9,1},... | collective-permute-start | bytes 393224 | tf_op jit(solution)/shard_map/ppermute | solution.py:93
  38.7 11.0 %collective-permute-start.7 = (bf16[256,256]{1,0:T(8,128)(2,1)S(1)}, bf16[256,256]{1,0:T(8,128)(2,1)S(1)}, u32[]{:S(2)}, u32[]{:S(2)}) collective-permute-start(bf16[256,256]{1,0:T(8,128)(2,1)S(1)} %get-tuple-element.41), channel_id=1, source_target_pairs={{0,16},{1,17},{2,18},{3,19},{4,20},{5,21},{6,22},{7,23},{8,24},{9,... | collective-permute-start | bytes 393224 | tf_op jit(solution)/shard_map/ppermute | solution.py:93
  41.1 8.6 %collective-permute-start.8 = (bf16[256,256]{1,0:T(8,128)(2,1)S(1)}, bf16[256,256]{1,0:T(8,128)(2,1)S(1)}, u32[]{:S(2)}, u32[]{:S(2)}) collective-permute-start(bf16[256,256]{1,0:T(8,128)(2,1)S(1)} %get-tuple-element.42), channel_id=1, source_target_pairs={{0,24},{1,25},{2,26},{3,27},{4,28},{5,29},{6,30},{7,31},{8,16},{9,... | collective-permute-start | bytes 393224 | tf_op jit(solution)/shard_map/ppermute | solution.py:93
  50.9 13.7 %collective-permute-start.15 = (f32[136,1024]{1,0:T(8,128)S(1)}, f32[136,1024]{1,0:T(8,128)S(1)}, u32[]{:S(2)}, u32[]{:S(2)}) collective-permute-start(f32[136,1024]{1,0:T(8,128)S(1)} %get-tuple-element.49), channel_id=1, source_target_pairs={{0,4},{1,5},{2,6},{3,7},{4,0},{5,1},{6,2},{7,3},{8,12},{9,13},{10,... | collective-permute-start | bytes 1671176 | tf_op jit(solution)/shard_map/ppermute | solution.py:93
  51.0 10.7 %collective-permute-start.1 = (bf16[192,1024]{1,0:T(8,128)(2,1)S(1)}, bf16[192,1024]{1,0:T(8,128)(2,1)S(1)}, u32[]{:S(2)}, u32[]{:S(2)}) collective-permute-start(bf16[192,1024]{1,0:T(8,128)(2,1)S(1)} %slice_dynamic-update-slice_fusion), channel_id=1, source_target_pairs={{0,2},{1,3},{2,0},{3,1},{4,5},{5,4},{6,7},{7,6},{8,10},{9,11},{10,... | collective-permute-start | bytes 1179656 | tf_op jit(solution)/shard_map/ppermute | solution.py:93
  57.1 4.7 %copy-start.2 = (bf16[1024]{0:T(1024)(128)(2,1)S(1)}, bf16[1024]{0:T(1024)(128)(2,1)}, u32[]{:S(2)}) copy-start(bf16[1024]{0:T(1024)(128)(2,1)} %bias_ref.1) | copy-start | bytes 6148

commit v4 on v3

--- a/solution.py
+++ b/solution.py
@@ -280,22 +280,26 @@
     return jnp.where(mine, low, high), jnp.where(mine, high, low)
 
 
-def early_kernel(m0, m1, m2, m3, cnear, cfar, e0, e1, e2, keep, give, pair, third):
+def early_kernel(m0, m1, m2, m3, cnear, cfar, ez, e0, e1, e2, keep, give, pair, third):
     mrows = cnear.shape[0] // 2
     f32 = jnp.float32
     ms = (m0, m1, m2, m3)
+    low, high = pl.ds(0, mrows), pl.ds(mrows, mrows)
+    near = [(e0, 0), (e0, 1), (e0, 2)]
+    hop = [(e1, 0), (e1, 1), (e1, 2)]
+    second = [(e2, 0), (e2, 1), (e2, 2)]
     lhs = []
     rhs = []
     sums = []
-    for j, (c, e) in enumerate(((cnear, e0), (cnear, e1), (cfar, e2), (cfar, None))):
-        rows = c[(j % 2) * mrows:(j % 2 + 1) * mrows, :]
-        count = 1 if e is None else MERGE
-        lhs += [m[j * mrows:(j + 1) * mrows, :] for m in ms[:count]]
-        rhs.append(rows)
-        if e is not None:
-            rhs.append(e[...])
-            b = [e[i * mrows:(i + 1) * mrows, :].astype(f32) for i in range(MERGE - 1)]
-            sums.append((rows.astype(f32) + b[0]) + (b[1] + b[2]))
+    for j, (c, at, parts) in enumerate(
+        ((cnear, low, near), (cnear, high, hop), (cfar, low, second), (cfar, high, [(ez, 0)]))
+    ):
+        blocks = [c[at, :]] + [e[i * mrows:(i + 1) * mrows, :] for e, i in parts]
+        lhs += [m[j * mrows:(j + 1) * mrows, :] for m in ms[:len(blocks)]]
+        rhs += blocks
+        if len(blocks) == MERGE:
+            b = [x.astype(f32) for x in blocks]
+            sums.append((b[0] + b[1]) + (b[2] + b[3]))
     total = lax.dot_general(
         jnp.concatenate(lhs, axis=0),
         jnp.concatenate(rhs, axis=0),
@@ -307,36 +311,35 @@
     third[...] = sums[2]
 
 
-def last_rows(ms, theirs, mrows):
+def last_rows(m2, m3, theirs):
     core = lax.axis_index("view") % 2
-    group = ms[0].shape[1] // 2
+    group = m2.shape[1] // 2
+    mrows = m2.shape[0] // SPANS
     start = pl.multiple_of((1 - core if theirs else core) * group, LANES)
     first = (SPANS - 1) * mrows
-    return jnp.concatenate([m[first:first + mrows, pl.ds(start, group)] for m in ms], axis=0)
-
-
-def give_kernel(m1, m2, m3, cfar, e3, give_in, pair, third, give, bias_out):
+    return jnp.concatenate(
+        [m[first:first + mrows, pl.ds(start, group)] for m in (m2, m3)], axis=0
+    )
+
+
+def give_kernel(m2, m3, cfar, ez, e3, give_in, pair, third, give, bias_out):
     mrows = cfar.shape[0] // 2
     group = give_in.shape[0]
     f32 = jnp.float32
     give[:group, :] = give_in[...] + lax.dot_general(
-        last_rows((m1, m2, m3), True, mrows),
-        e3[...],
-        (((0,), (0,)), ((), ())),
-        preferred_element_type=f32,
-    )
-    b = [e3[i * mrows:(i + 1) * mrows, :].astype(f32) for i in range(MERGE - 1)]
-    fourth = (cfar[mrows:, :].astype(f32) + b[0]) + (b[1] + b[2])
+        last_rows(m2, m3, True), e3[...], (((0,), (0,)), ((), ())), preferred_element_type=f32
+    )
+    b = [e3[i * mrows:(i + 1) * mrows, :].astype(f32) for i in range(2)]
+    fourth = (cfar[mrows:, :].astype(f32) + ez[...].astype(f32)) + (b[0] + b[1])
     tree = pair[...] + (third[...] + fourth)
     bias = jnp.broadcast_to(jnp.sum(tree, axis=0, keepdims=True), bias_out.shape)
     bias_out[...] = bias
     give[group:, :] = bias
 
 
-def keep_kernel(m1, m2, m3, e3, keep_in, keep):
-    mrows = e3.shape[0] // (MERGE - 1)
+def keep_kernel(m2, m3, e3, keep_in, keep):
     keep[...] = keep_in[...] + lax.dot_general(
-        last_rows((m1, m2, m3), False, mrows),
+        last_rows(m2, m3, False),
         e3[...],
         (((0,), (0,)), ((), ())),
         preferred_element_type=jnp.float32,
@@ -416,8 +419,9 @@
     cfar = hop(cnear, span_offset=second)
     extra = jnp.concatenate(zs, axis=0)
     e1 = hop(extra, span_offset=first)
+    ez = hop(cfar[mrows:], view_offset=2)
     e2 = hop(extra, span_offset=second)
-    e3 = hop(e1, span_offset=second)
+    e3 = hop(e1[mrows:], span_offset=second)
     picks = call(
         select_kernel,
         (scan_order, tv, q_near, q_far),
@@ -457,20 +461,20 @@
     wide = shape(group, width, f32)
     keep, give, pair, third = call(
         early_kernel,
-        (*ms, cnear, cfar, extra, e1, e2),
+        (*ms, cnear, cfar, ez, extra, e1, e2),
         [wide, wide] + [shape(mrows, width, f32)] * 2,
         cost_of(4 * spans * tok_dev * group * width, 8 * tok_dev * width),
     )
     give, keep_bias = call(
         give_kernel,
-        (*ms[1:], cfar, e3, give, pair, third),
+        (*ms[2:], cfar, ez, e3, give, pair, third),
         [shape(group + 8, width, f32), shape(8, width, f32)],
         cost_of(2 * tok_dev * group * width, 4 * tok_dev * width),
     )
     taken = hop(give, view_offset=1)
     (keep,) = call(
         keep_kernel,
-        (*ms[1:], e3, keep),
+        (*ms[2:], e3, keep),
         [wide],
         cost_of(2 * tok_dev * group * width, 4 * tok_dev * width),
     )

time: 65.6 us -> 68.1 us (1.038); the launches traced: 65.4 us -> 66.8 us
  starting transfers between devices: 22.4 us -> 23.4 us
    ppermute x16 -> x17, starting transfers between devices: 22.4 us -> 23.4 us  [xor_permute(): return lax.ppermute(x, ('view', 'span'), pairs)]
    ppermute x16 -> x17, waiting for transfers between devices: 24.6 us -> 25 us  [xor_permute(): return lax.ppermute(x, ('view', 'span'), pairs)]
  transfers between devices with their start and end apart: 16 -> 17, of which waited for: 4 -> 4; matrix products, arithmetic and copies ran while one was open for 0% -> 0% of each run, Pallas kernels for 22% -> 22%
where the time goes in v4:
time: 68.1 us; the launch traced here: 66.8 us
  waiting for transfers between devices  25 us (37%)
  starting transfers between devices  23.4 us (34%)
  Pallas kernels  15.6 us (23%)
  local copies, waits for them, and re-layouts  2.05 us (3%)
  between operations  0.83 us (1%)
    ppermute x17, waiting for transfers between devices, xor_permute(): return lax.ppermute(x, ('view', 'span'), pairs)  25 us
    ppermute x17, starting transfers between devices, xor_permute(): return lax.ppermute(x, ('view', 'span'), pairs)  23.4 us
    pallas_call x13, Pallas kernels, call(): pl.pallas_call(kernel, out_shape=outs, in_specs=[far if i in hbm else vme...  15.6 us
    unnamed x10, local copies, waits for them, and re-layouts  1.97 us
  transfers between devices with their start and end apart: 17, of which 4 were waited for; matrix products, arithmetic and copies ran while one was open for 0% of the time, Pallas kernels for 22%

profile of v4, /device:TPU:0, one launch (start us, length us, event | category | flops | bytes accessed | tf_op | source)
XLA Modules:
  0.0 66.8 jit_solution(9047958263943761435)
XLA Ops:
  0.6 3.1 %collective-permute-start.8 = (bf16[64,1024]{1,0:T(8,128)(2,1)}, bf16[64,1024]{1,0:T(8,128)(2,1)S(1)}, u32[]{:S(2)}, u32[]{:S(2)}) collective-permute-start(bf16[64,1024]{1,0:T(8,128)(2,1)} %bitcast.6), channel_id=1, source_target_pairs={{0,8},{1,9},{2,10},{3,11},{4,12},{5,13},{6,14},{7,15},{8,0},{9,1},... | collective-permute-start | bytes 393224 | tf_op jit(solution)/shard_map/ppermute | solution.py:93
  3.7 2.6 %collective-permute-start.9 = (bf16[64,1024]{1,0:T(8,128)(2,1)}, bf16[64,1024]{1,0:T(8,128)(2,1)S(1)}, u32[]{:S(2)}, u32[]{:S(2)}) collective-permute-start(bf16[64,1024]{1,0:T(8,128)(2,1)} %bitcast.7), channel_id=1, source_target_pairs={{0,16},{1,17},{2,18},{3,19},{4,20},{5,21},{6,22},{7,23},{8,24},{9,... | collective-permute-start | bytes 393224 | tf_op jit(solution)/shard_map/ppermute | solution.py:93
  6.3 1.5 %collective-permute-start.2 = (bf16[64,1024]{1,0:T(8,128)(2,1)}, bf16[64,1024]{1,0:T(8,128)(2,1)S(1)}, u32[]{:S(2)}, u32[]{:S(2)}) collective-permute-start(bf16[64,1024]{1,0:T(8,128)(2,1)} %bitcast.8), channel_id=1, source_target_pairs={{0,1},{1,0},{2,3},{3,2},{4,6},{5,7},{6,4},{7,5},{8,9},{9,8},{10,11... | collective-permute-start | bytes 393224 | tf_op jit(solution)/shard_map/ppermute | solution.py:93
  7.8 0.2 collective-permute-start.10
  8.1 1.0 %copy-done = bf16[1,256,1024]{2,1,0:T(8,128)(2,1)S(1)} copy-done((bf16[1,256,1024]{2,1,0:T(8,128)(2,1)S(1)}, bf16[1,256,1024]{2,1,0:T(8,128)(2,1)}, u32[]{:S(2)}) %copy-start) | copy-done | bytes 524312
  9.1 0.1 shard_map.84
  9.2 0.4 collective-permute-start.4
  9.6 0.9 %copy-done.1 = bf16[1,64,1024]{2,1,0:T(8,128)(2,1)S(1)} copy-done((bf16[1,64,1024]{2,1,0:T(8,128)(2,1)S(1)}, bf16[1,64,1024]{2,1,0:T(8,128)(2,1)}, u32[]{:S(2)}) %copy-start.1) | copy-done | bytes 131096
  10.5 0.0 collective-permute-done.8
  10.6 5.8 %collective-permute-done.9 = bf16[64,1024]{1,0:T(8,128)(2,1)S(1)} collective-permute-done((bf16[64,1024]{1,0:T(8,128)(2,1)}, bf16[64,1024]{1,0:T(8,128)(2,1)S(1)}, u32[]{:S(2)}, u32[]{:S(2)}) %collective-permute-start.9) | collective-permute-done | bytes 131104 | tf_op jit(solution)/shard_map/ppermute | solution.py:93
  16.4 0.0 collective-permute-done.10
  16.4 1.6 %collective-permute-start.11 = (bf16[192,1024]{1,0:T(8,128)(2,1)S(1)}, bf16[192,1024]{1,0:T(8,128)(2,1)S(1)}, u32[]{:S(2)}, u32[]{:S(2)}) collective-permute-start(bf16[192,1024]{1,0:T(8,128)(2,1)S(1)} %constant_dynamic-update-slice_fusion.e0), channel_id=1, source_target_pairs={{0,1},{1,0},{2,3},{3,2},{4,6},{5,7},{6,4},{7,5},{8,9},{9,8},{10,11... | collective-permute-start | bytes 1179656 | tf_op jit(solution)/shard_map/ppermute | solution.py:93
  17.9 2.0 %collective-permute-start.15 = (bf16[192,1024]{1,0:T(8,128)(2,1)S(1)}, bf16[192,1024]{1,0:T(8,128)(2,1)S(1)}, u32[]{:S(2)}, u32[]{:S(2)}) collective-permute-start(bf16[192,1024]{1,0:T(8,128)(2,1)S(1)} %constant_dynamic-update-slice_fusion.e0), channel_id=1, source_target_pairs={{0,2},{1,3},{2,0},{3,1},{4,5},{5,4},{6,7},{7,6},{8,10},{9,11},{10,... | collective-permute-start | bytes 1179656 | tf_op jit(solution)/shard_map/ppermute | solution.py:93
  20.0 0.0 collective-permute-done.2
  20.0 0.1 collective-permute-start.3
  20.1 0.0 collective-permute-done.4.q_near
  20.1 2.1 %collective-permute-start.5 = (bf16[128,1024]{1,0:T(8,128)(2,1)S(1)}, bf16[128,1024]{1,0:T(8,128)(2,1)S(1)}, u32[]{:S(2)}, u32[]{:S(2)}) collective-permute-start(bf16[128,1024]{1,0:T(8,128)(2,1)S(1)} %slice_dynamic-update-slice_fusion.1), channel_id=1, source_target_pairs={{0,2},{1,3},{2,0},{3,1},{4,5},{5,4},{6,7},{7,6},{8,10},{9,11},{10,... | collective-permute-start | bytes 786440 | tf_op jit(solution)/shard_map/ppermute | solution.py:93
  22.2 0.8 %shard_map.85 = (bf16[192,1024]{1,0:T(8,128)(2,1)S(1)}, bf16[192,1024]{1,0:T(8,128)(2,1)S(1)}) custom-call(s32[1,1024]{1,0:T(1,128)S(1)} %copy-done.3, bf16[256,1024]{1,0:T(8,128)(2,1)S(1)} %get-tuple-element.28.t_ref), custom_call_target="tpu_custom_call" | custom-call | flops 150994944 | bytes 1048576 | tf_op jit(solution)/shard_map/pallas_call | solution.py:362
  22.9 0.6 collective-permute-start
  23.5 9.2 %collective-permute-done.3.far.cfar = bf16[128,1024]{1,0:T(8,128)(2,1)S(1)} collective-permute-done((bf16[128,1024]{1,0:T(8,128)(2,1)S(1)}, bf16[128,1024]{1,0:T(8,128)(2,1)S(1)}, u32[]{:S(2)}, u32[]{:S(2)}) %collective-permute-start.3) | collective-permute-done | bytes 262176 | tf_op jit(solution)/shard_map/ppermute | solution.py:93
  32.8 3.6 %collective-permute-start.14 = (bf16[64,1024]{1,0:T(8,128)(2,1)S(1)}, bf16[64,1024]{1,0:T(8,128)(2,1)S(1)}, u32[]{:S(2)}, u32[]{:S(2)}) collective-permute-start(bf16[64,1024]{1,0:T(8,128)(2,1)S(1)} %slice.19), channel_id=1, source_target_pairs={{0,8},{1,9},{2,10},{3,11},{4,12},{5,13},{6,14},{7,15},{8,0},{9,1},... | collective-permute-start | bytes 393224 | tf_op jit(solution)/shard_map/ppermute | solution.py:93
  36.3 0.0 collective-permute-done.11.e1
  36.4 1.1 %collective-permute-start.12 = (bf16[128,1024]{1,0:T(8,128)(2,1)S(1)}, bf16[128,1024]{1,0:T(8,128)(2,1)S(1)}, u32[]{:S(2)}, u32[]{:S(2)}) collective-permute-start(bf16[128,1024]{1,0:T(8,128)(2,1)S(1)} %slice.18), channel_id=1, source_target_pairs={{0,2},{1,3},{2,0},{3,1},{4,5},{5,4},{6,7},{7,6},{8,10},{9,11},{10,... | collective-permute-start | bytes 786440 | tf_op jit(solution)/shard_map/ppermute | solution.py:93
  37.4 0.0 collective-permute-done.5.q_far
  37.4 0.7 %shard_map.92 = (bf16[256,256]{1,0:T(8,128)(2,1)S(1)}, bf16[256,256]{1,0:T(8,128)(2,1)S(1)}, bf16[256,256]{1,0:T(8,128)(2,1)S(1)}, bf16[256,256]{1,0:T(8,128)(2,1)S(1)}) custom-call(s32[1,1024]{1,0:T(1,128)S(1)} %copy-done.3, bf16[256,1024]{1,0:T(8,128)(2,1)S(1)} %get-tuple-element.28.t_ref, bf16[128,1024]{1,0:T(8,128)(2,1)S(1)} %collective-permute-done.4.q_near, ...), custom_call_target="tpu_custom_call" | custom-call | flops 536870912 | bytes 1048576 | tf_op jit(solution)/shard_map/pallas_call | solution.py:362
  38.2 2.4 %collective-permute-start.6 = (bf16[256,256]{1,0:T(8,128)(2,1)S(1)}, bf16[256,256]{1,0:T(8,128)(2,1)S(1)}, u32[]{:S(2)}, u32[]{:S(2)}) collective-permute-start(bf16[256,256]{1,0:T(8,128)(2,1)S(1)} %get-tuple-element.40), channel_id=1, source_target_pairs={{0,16},{1,17},{2,18},{3,19},{4,20},{5,21},{6,22},{7,23},{8,24},{9,... | collective-permute-start | bytes 393224 | tf_op jit(solution)/shard_map/ppermute | solution.py:93
  40.6 0.0 collective-permute-done.14.ez
  40.6 1.7 %collective-permute-start.7 = (bf16[256,256]{1,0:T(8,128)(2,1)S(1)}, bf16[256,256]{1,0:T(8,128)(2,1)S(1)}, u32[]{:S(2)}, u32[]{:S(2)}) collective-permute-start(bf16[256,256]{1,0:T(8,128)(2,1)S(1)} %get-tuple-element.41), channel_id=1, source_target_pairs={{0,24},{1,25},{2,26},{3,27},{4,28},{5,29},{6,30},{7,31},{8,16},{9,... | collective-permute-start | bytes 393224 | tf_op jit(solution)/shard_map/ppermute | solution.py:93
  42.2 0.0 collective-permute-done.15.e2
  42.2 0.3 collective-permute-start.13
  42.5 8.7 %collective-permute-done.6.m2 = bf16[256,256]{1,0:T(8,128)(2,1)S(1)} collective-permute-done((bf16[256,256]{1,0:T(8,128)(2,1)S(1)}, bf16[256,256]{1,0:T(8,128)(2,1)S(1)}, u32[]{:S(2)}, u32[]{:S(2)}) %collective-permute-start.6) | collective-permute-done | bytes 131104 | tf_op jit(solution)/shard_map/ppermute | solution.py:93
  51.2 0.0 collective-permute-done.7.m3
  51.2 1.3 %collective-permute-done.13.m1 = bf16[256,256]{1,0:T(8,128)(2,1)S(1)} collective-permute-done((bf16[256,256]{1,0:T(8,128)(2,1)S(1)}, bf16[256,256]{1,0:T(8,128)(2,1)S(1)}, u32[]{:S(2)}, u32[]{:S(2)}) %collective-permute-start.13) | collective-permute-done | bytes 131104 | tf_op jit(solution)/shard_map/ppermute | solution.py:93
  52.5 0.8 %shard_map.93 = (f32[128,1024]{1,0:T(8,128)S(1)}, f32[128,1024]{1,0:T(8,128)S(1)}, f32[64,1024]{1,0:T(8,128)S(1)}, f32[64,1024]{1,0:T(8,128)S(1)}) custom-call(bf16[256,256]{1,0:T(8,128)(2,1)S(1)} %get-tuple-element.42.m0, bf16[256,256]{1,0:T(8,128)(2,1)S(1)} %collective-permute-done.13.m1, bf16[256,256]{1,0:T(8,128)(2,1)S(1)} %collective-permute-done.6.m2, ...), custom_call_target="tpu_custom_call" | custom-call | flops 536870912 | bytes 2097152 | tf_op jit(solution)/shard_map/pallas_call | solution.py:362
  53.3 0.0 collective-permute-done.12.e3
  53.3 0.3 shard_map.95
  53.7 0.1 collective-permute-start.16
  53.7 0.0 collective-permute-done.p_near
  53.8 0.2 collective-permute-start.1
  54.0 2.2 %shard_map.87 = (bf16[1024,1024]{1,0:T(8,128)(2,1)S(1)}, bf16[1024,1024]{1,0:T(8,128)(2,1)S(1)}) custom-call(bf16[4096,1024]{1,0:T(8,128)(2,1)} %w_hbm.3), custom_call_target="tpu_custom_call" | custom-call | flops 1024 | bytes 4194304 | tf_op jit(solution)/shard_map/pallas_call | solution.py:362
  56.2 2.2 %shard_map.88 = (bf16[1024,1024]{1,0:T(8,128)(2,1)S(1)}, bf16[1024,1024]{1,0:T(8,128)(2,1)S(1)}) custom-call(bf16[4096,1024]{1,0:T(8,128)(2,1)} %w_hbm.3), custom_call_target="tpu_custom_call" | custom-call | flops 1024 | bytes 4194304 | tf_op jit(solution)/shard_map/pallas_call | solution.py:362
  58.5 3.7 %shard_map.91 = bf16[256,1024]{1,0:T(8,128)(2,1)} custom-call(s32[1,1024]{1,0:T(1,128)S(1)} %copy-done.3, bf16[128,1024]{1,0:T(8,128)(2,1)S(1)} %constant_dynamic-update-slice_fusion.3.near.cnear, bf16[128,1024]{1,0:T(8,128)(2,1)S(1)} %collective-permute-done.3.far.cfar, bf16[1024,1024]{1,0:T(8,128)(2,1)S(1)} %get-tuple-element.34.w0, ...), custom_call_target="tpu_custom_call" | custom-call | flops 2684354560 | bytes 8388608 | tf_op jit(solution)/shard_map/pallas_call | solution.py:362
  62.2 0.9 %shard_map.86 = (f32[256,1024]{1,0:T(8,128)S(1)}, bf16[256,96]{1,0:T(8,128)(2,1)S(1)}, bf16[256,96]{1,0:T(8,128)(2,1)S(1)}) custom-call(s32[1,1024]{1,0:T(1,128)S(1)} %copy-done.3, bf16[256,1024]{1,0:T(8,128)(2,1)S(1)} %get-tuple-element.28.t_ref, bf16[192,1024]{1,0:T(8,128)(2,1)S(1)} %collective-permute-done.p_near), custom_call_target="tpu_custom_call" | custom-call | flops 268435456 | bytes 1048576 | tf_op jit(solution)/shard_map/pallas_call | solution.py:362
  63.1 0.3 shard_map.94.keep
  63.4 0.0 collective-permute-done.1.p_far
  63.4 2.5 %shard_map.89 = bf16[64,1024]{1,0:T(8,128)(2,1)} custom-call(bf16[1024]{0:T(1024)(128)(2,1)S(1)} %copy-done.2, f32[256,1024]{1,0:T(8,128)S(1)} %get-tuple-element.30.mine_ref, bf16[256,96]{1,0:T(8,128)(2,1)S(1)} %get-tuple-element.31.hot_g, bf16[256,96]{1,0:T(8,128)(2,1)S(1)} %get-tuple-element.32.hot_d, bf16[192,1024]{1,0:T(8,128)(2,1)S(1)} %collective-permute-done.1.p_far, ...), custom_call_target="tpu_custom_call" | custom-call | flops 1073741824 | bytes 8388608 | tf_op jit(solution)/shard_map/pallas_call | solution.py:362
  66.0 0.0 collective-permute-done.16.taken
  66.0 0.9 %shard_map.96 = (f32[128,1024]{1,0:T(8,128)}, f32[1,1024]{1,0:T(1,128)}) custom-call(f32[128,1024]{1,0:T(8,128)S(1)} %shard_map.94.keep, f32[8,1024]{1,0:T(8,128)S(1)} %get-tuple-element.48.keep_bias, f32[136,1024]{1,0:T(8,128)S(1)} %collective-permute-done.16.taken), custom_call_target="tpu_custom_call" | custom-call | flops 131072 | bytes 1572864 | tf_op jit(solution)/shard_map/pallas_call | solution.py:362
  (15 shorter events, 0.1 us)
Async XLA Ops:
  0.6 9.9 %collective-permute-start.8 = (bf16[64,1024]{1,0:T(8,128)(2,1)}, bf16[64,1024]{1,0:T(8,128)(2,1)S(1)}, u32[]{:S(2)}, u32[]{:S(2)}) collective-permute-start(bf16[64,1024]{1,0:T(8,128)(2,1)} %bitcast.6), channel_id=1, source_target_pairs={{0,8},{1,9},{2,10},{3,11},{4,12},{5,13},{6,14},{7,15},{8,0},{9,1},... | collective-permute-start | bytes 393224 | tf_op jit(solution)/shard_map/ppermute | solution.py:93
  3.7 12.6 %collective-permute-start.9 = (bf16[64,1024]{1,0:T(8,128)(2,1)}, bf16[64,1024]{1,0:T(8,128)(2,1)S(1)}, u32[]{:S(2)}, u32[]{:S(2)}) collective-permute-start(bf16[64,1024]{1,0:T(8,128)(2,1)} %bitcast.7), channel_id=1, source_target_pairs={{0,16},{1,17},{2,18},{3,19},{4,20},{5,21},{6,22},{7,23},{8,24},{9,... | collective-permute-start | bytes 393224 | tf_op jit(solution)/shard_map/ppermute | solution.py:93
  6.3 13.6 %collective-permute-start.2 = (bf16[64,1024]{1,0:T(8,128)(2,1)}, bf16[64,1024]{1,0:T(8,128)(2,1)S(1)}, u32[]{:S(2)}, u32[]{:S(2)}) collective-permute-start(bf16[64,1024]{1,0:T(8,128)(2,1)} %bitcast.8), channel_id=1, source_target_pairs={{0,1},{1,0},{2,3},{3,2},{4,6},{5,7},{6,4},{7,5},{8,9},{9,8},{10,11... | collective-permute-start | bytes 393224 | tf_op jit(solution)/shard_map/ppermute | solution.py:93
  7.8 8.5 %collective-permute-start.10 = (bf16[64,1024]{1,0:T(8,128)(2,1)}, bf16[64,1024]{1,0:T(8,128)(2,1)S(1)}, u32[]{:S(2)}, u32[]{:S(2)}) collective-permute-start(bf16[64,1024]{1,0:T(8,128)(2,1)} %bitcast.9), channel_id=1, source_target_pairs={{0,24},{1,25},{2,26},{3,27},{4,28},{5,29},{6,30},{7,31},{8,16},{9,... | collective-permute-start | bytes 393224 | tf_op jit(solution)/shard_map/ppermute | solution.py:93
  8.1 1.0 %copy-start = (bf16[1,256,1024]{2,1,0:T(8,128)(2,1)S(1)}, bf16[1,256,1024]{2,1,0:T(8,128)(2,1)}, u32[]{:S(2)}) copy-start(bf16[1,256,1024]{2,1,0:T(8,128)(2,1)} %param.5) | copy-start | bytes 1572868
  9.1 13.1 %copy-start.3 = (s32[1,1024]{1,0:T(1,128)S(1)}, s32[1,1024]{1,0:T(1,128)}, u32[]{:S(2)}) copy-start(s32[1,1024]{1,0:T(1,128)} %order_ref.7) | copy-start | bytes 12292
  9.2 10.8 %collective-permute-start.4 = (bf16[128,1024]{1,0:T(8,128)(2,1)S(1)}, bf16[128,1024]{1,0:T(8,128)(2,1)S(1)}, u32[]{:S(2)}, u32[]{:S(2)}) collective-permute-start(bf16[128,1024]{1,0:T(8,128)(2,1)S(1)} %get-tuple-element.38), channel_id=1, source_target_pairs={{0,1},{1,0},{2,3},{3,2},{4,6},{5,7},{6,4},{7,5},{8,9},{9,8},{10,11... | collective-permute-start | bytes 786440 | tf_op jit(solution)/shard_map/ppermute | solution.py:93
  9.6 0.9 %copy-start.1 = (bf16[1,64,1024]{2,1,0:T(8,128)(2,1)S(1)}, bf16[1,64,1024]{2,1,0:T(8,128)(2,1)}, u32[]{:S(2)}) copy-start(bf16[1,64,1024]{2,1,0:T(8,128)(2,1)} %param.9) | copy-start | bytes 393220
  16.4 20.0 %collective-permute-start.11 = (bf16[192,1024]{1,0:T(8,128)(2,1)S(1)}, bf16[192,1024]{1,0:T(8,128)(2,1)S(1)}, u32[]{:S(2)}, u32[]{:S(2)}) collective-permute-start(bf16[192,1024]{1,0:T(8,128)(2,1)S(1)} %constant_dynamic-update-slice_fusion.e0), channel_id=1, source_target_pairs={{0,1},{1,0},{2,3},{3,2},{4,6},{5,7},{6,4},{7,5},{8,9},{9,8},{10,11... | collective-permute-start | bytes 1179656 | tf_op jit(solution)/shard_map/ppermute | solution.py:93
  17.9 24.3 %collective-permute-start.15 = (bf16[192,1024]{1,0:T(8,128)(2,1)S(1)}, bf16[192,1024]{1,0:T(8,128)(2,1)S(1)}, u32[]{:S(2)}, u32[]{:S(2)}) collective-permute-start(bf16[192,1024]{1,0:T(8,128)(2,1)S(1)} %constant_dynamic-update-slice_fusion.e0), channel_id=1, source_target_pairs={{0,2},{1,3},{2,0},{3,1},{4,5},{5,4},{6,7},{7,6},{8,10},{9,11},{10,... | collective-permute-start | bytes 1179656 | tf_op jit(solution)/shard_map/ppermute | solution.py:93
  20.0 12.8 %collective-permute-start.3 = (bf16[128,1024]{1,0:T(8,128)(2,1)S(1)}, bf16[128,1024]{1,0:T(8,128)(2,1)S(1)}, u32[]{:S(2)}, u32[]{:S(2)}) collective-permute-start(bf16[128,1024]{1,0:T(8,128)(2,1)S(1)} %constant_dynamic-update-slice_fusion.3.near.cnear), channel_id=1, source_target_pairs={{0,2},{1,3},{2,0},{3,1},{4,5},{5,4},{6,7},{7,6},{8,10},{9,11},{10,... | collective-permute-start | bytes 786440 | tf_op jit(solution)/shard_map/ppermute | solution.py:93
  20.1 17.4 %collective-permute-start.5 = (bf16[128,1024]{1,0:T(8,128)(2,1)S(1)}, bf16[128,1024]{1,0:T(8,128)(2,1)S(1)}, u32[]{:S(2)}, u32[]{:S(2)}) collective-permute-start(bf16[128,1024]{1,0:T(8,128)(2,1)S(1)} %slice_dynamic-update-slice_fusion.1), channel_id=1, source_target_pairs={{0,2},{1,3},{2,0},{3,1},{4,5},{5,4},{6,7},{7,6},{8,10},{9,11},{10,... | collective-permute-start | bytes 786440 | tf_op jit(solution)/shard_map/ppermute | solution.py:93
  22.9 30.8 %collective-permute-start = (bf16[192,1024]{1,0:T(8,128)(2,1)S(1)}, bf16[192,1024]{1,0:T(8,128)(2,1)S(1)}, u32[]{:S(2)}, u32[]{:S(2)}) collective-permute-start(bf16[192,1024]{1,0:T(8,128)(2,1)S(1)} %get-tuple-element.29), channel_id=1, source_target_pairs={{0,1},{1,0},{2,3},{3,2},{4,6},{5,7},{6,4},{7,5},{8,9},{9,8},{10,11... | collective-permute-start | bytes 1179656 | tf_op jit(solution)/shard_map/ppermute | solution.py:93
  32.8 7.8 %collective-permute-start.14 = (bf16[64,1024]{1,0:T(8,128)(2,1)S(1)}, bf16[64,1024]{1,0:T(8,128)(2,1)S(1)}, u32[]{:S(2)}, u32[]{:S(2)}) collective-permute-start(bf16[64,1024]{1,0:T(8,128)(2,1)S(1)} %slice.19), channel_id=1, source_target_pairs={{0,8},{1,9},{2,10},{3,11},{4,12},{5,13},{6,14},{7,15},{8,0},{9,1},... | collective-permute-start | bytes 393224 | tf_op jit(solution)/shard_map/ppermute | solution.py:93
  36.4 16.9 %collective-permute-start.12 = (bf16[128,1024]{1,0:T(8,128)(2,1)S(1)}, bf16[128,1024]{1,0:T(8,128)(2,1)S(1)}, u32[]{:S(2)}, u32[]{:S(2)}) collective-permute-start(bf16[128,1024]{1,0:T(8,128)(2,1)S(1)} %slice.18), channel_id=1, source_target_pairs={{0,2},{1,3},{2,0},{3,1},{4,5},{5,4},{6,7},{7,6},{8,10},{9,11},{10,... | collective-permute-start | bytes 786440 | tf_op jit(solution)/shard_map/ppermute | solution.py:93
  38.2 13.0 %collective-permute-start.6 = (bf16[256,256]{1,0:T(8,128)(2,1)S(1)}, bf16[256,256]{1,0:T(8,128)(2,1)S(1)}, u32[]{:S(2)}, u32[]{:S(2)}) collective-permute-start(bf16[256,256]{1,0:T(8,128)(2,1)S(1)} %get-tuple-element.40), channel_id=1, source_target_pairs={{0,16},{1,17},{2,18},{3,19},{4,20},{5,21},{6,22},{7,23},{8,24},{9,... | collective-permute-start | bytes 393224 | tf_op jit(solution)/shard_map/ppermute | solution.py:93
  40.6 10.7 %collective-permute-start.7 = (bf16[256,256]{1,0:T(8,128)(2,1)S(1)}, bf16[256,256]{1,0:T(8,128)(2,1)S(1)}, u32[]{:S(2)}, u32[]{:S(2)}) collective-permute-start(bf16[256,256]{1,0:T(8,128)(2,1)S(1)} %get-tuple-element.41), channel_id=1, source_target_pairs={{0,24},{1,25},{2,26},{3,27},{4,28},{5,29},{6,30},{7,31},{8,16},{9,... | collective-permute-start | bytes 393224 | tf_op jit(solution)/shard_map/ppermute | solution.py:93
  42.2 10.3 %collective-permute-start.13 = (bf16[256,256]{1,0:T(8,128)(2,1)S(1)}, bf16[256,256]{1,0:T(8,128)(2,1)S(1)}, u32[]{:S(2)}, u32[]{:S(2)}) collective-permute-start(bf16[256,256]{1,0:T(8,128)(2,1)S(1)} %get-tuple-element.43), channel_id=1, source_target_pairs={{0,8},{1,9},{2,10},{3,11},{4,12},{5,13},{6,14},{7,15},{8,0},{9,1},... | collective-permute-start | bytes 393224 | tf_op jit(solution)/shard_map/ppermute | solution.py:93
  53.7 12.3 %collective-permute-start.16 = (f32[136,1024]{1,0:T(8,128)S(1)}, f32[136,1024]{1,0:T(8,128)S(1)}, u32[]{:S(2)}, u32[]{:S(2)}) collective-permute-start(f32[136,1024]{1,0:T(8,128)S(1)} %get-tuple-element.49), channel_id=1, source_target_pairs={{0,4},{1,5},{2,6},{3,7},{4,0},{5,1},{6,2},{7,3},{8,12},{9,13},{10,... | collective-permute-start | bytes 1671176 | tf_op jit(solution)/shard_map/ppermute | solution.py:93
  53.8 9.6 %collective-permute-start.1 = (bf16[192,1024]{1,0:T(8,128)(2,1)S(1)}, bf16[192,1024]{1,0:T(8,128)(2,1)S(1)}, u32[]{:S(2)}, u32[]{:S(2)}) collective-permute-start(bf16[192,1024]{1,0:T(8,128)(2,1)S(1)} %slice_dynamic-update-slice_fusion), channel_id=1, source_target_pairs={{0,2},{1,3},{2,0},{3,1},{4,5},{5,4},{6,7},{7,6},{8,10},{9,11},{10,... | collective-permute-start | bytes 1179656 | tf_op jit(solution)/shard_map/ppermute | solution.py:93
  62.2 1.2 %copy-start.2 = (bf16[1024]{0:T(1024)(128)(2,1)S(1)}, bf16[1024]{0:T(1024)(128)(2,1)}, u32[]{:S(2)}) copy-start(bf16[1024]{0:T(1024)(128)(2,1)} %bias_ref.1) | copy-start | bytes 6148
